TPU v7x, 1024 devices: a whole 4x4x32 slice. The times are simulated.
1024 devices in a mesh: section: 16 (over y, x), expert: 64 (over z, core).
Axes of the slice: x: 4, y: 4, z: 32, core: 2. Of those that a mesh axis runs over, the one named last changes fastest.
Arguments:
- cotangent: bfloat16 [131072, 4096], P(('section', 'expert')), may hold values from -6 to 6
- expert_ids: int32 [131072, 1], P(('section', 'expert')), may hold values from 0 to 63; in each aligned block of 128 rows (0 to 127, 128 to 255, ...) at most 4 rows name the same one
- route_weight: float32 [131072], P(('section', 'expert')), may hold values from 0.1 to 1
- saved_preact: bfloat16 [131072, 2048], P(('section', 'expert')), may hold values from -6 to 6
- down_weight: bfloat16 [64, 1024, 4096], P('expert'), may hold values from -0.09375 to 0.09375
Outputs:
- d_preact: bfloat16 [131072, 2048], P(('section', 'expert'))
- d_route: float32 [131072], P(('section', 'expert'))
Inputs may be any that keep to these rules, and one draw needn't show every extreme that they name: `expert_ids`: at most 4 of the 128 tokens of one device name the same expert, and on some devices one expert is named by exactly 4 of them.
All inputs are finite; a program needn't handle non-finite values.
Results may differ from a plain program's by a relative error of at most 0.0049.
Values may be sent and summed in bfloat16 or wider, within the bound.
No kernel may reach another device: no remote copies, remote signals or barrier semaphores. Data moves between devices by JAX's collectives and lax.ppermute only.
A program may use at most 32 MiB of HBM per device.

v0:
```python
import jax
import jax.numpy as jnp
from jax import lax
from jax.sharding import PartitionSpec as P


SLOTS = 4
NEAR = 4
PAIR = 2 * SLOTS
CELL = 2 * PAIR
BLOCK = NEAR * CELL
PACKED = 48
PARTS = 2
NOTES = 128


def moved(block, section_step=0, chip_step=0, flip=False):
    experts = lax.axis_size("expert")
    chips = experts // 2

    def target(place):
        chip, core = divmod(place, 2)
        step = -chip_step if core else chip_step
        return ((chip + step) % chips) * 2 + (1 - core if flip else core)

    if not section_step:
        return lax.ppermute(block, "expert", [(i, target(i)) for i in range(experts)])
    sections = lax.axis_size("section")
    route = [
        (s * experts + i, ((s + section_step) % sections) * experts + target(i))
        for s in range(sections)
        for i in range(experts)
    ]
    return lax.ppermute(block, ("section", "expert"), route)


def numbers(count):
    return jnp.arange(count, dtype=jnp.int32)


def onehot(left, right):
    return (left[:, None] == right[None, :]).astype(jnp.bfloat16)


def picked(selection, rows):
    return jnp.dot(selection, rows, preferred_element_type=jnp.float32).astype(jnp.bfloat16)


def expert_products(rows, weight):
    dims = (((1,), (1,)), ((), ()))
    return lax.dot_general(rows, weight, dims, preferred_element_type=jnp.float32).astype(
        jnp.bfloat16
    )


def ranked(expert):
    place = numbers(expert.shape[0])
    same = (expert[:, None] == expert[None, :]) & (place[None, :] < place[:, None])
    return jnp.sum(same.astype(jnp.int32), axis=1)


def direct(rows, expert, rank, weight):
    experts = lax.axis_size("expert")
    slot = expert * SLOTS + rank
    places = numbers(experts * SLOTS)
    send = picked(onehot(places, slot), rows)
    received = lax.all_to_all(send, "expert", split_axis=0, concat_axis=0, tiled=True)
    products = expert_products(received, weight)
    returned = lax.all_to_all(products, "expert", split_axis=0, concat_axis=0, tiled=True)
    return picked(onehot(slot, places), returned)


def noted(rows, slot, flag):
    column = lax.broadcasted_iota(jnp.int32, (rows.shape[0], NOTES), 1)
    notes = jnp.where(column == 0, slot[:, None], jnp.where(column == 1, flag, 0))
    return jnp.concatenate([rows, notes.astype(jnp.bfloat16)], axis=1)


def packed(rows, far_rows, expert, far_expert, rank, weight):
    wide = rows.shape[1]
    experts = lax.axis_size("expert")
    chips = experts // 2
    half = chips // 2
    blocks = half // NEAR
    place = lax.axis_index("expert")
    chip, core = place // 2, place % 2
    tokens = expert.shape[0]

    both = jnp.concatenate([expert, far_expert])
    source = numbers(2 * tokens) // tokens
    ranks = jnp.concatenate([rank, ranked(far_expert)])
    crossing = (both + core) % 2
    ahead = (both // 2 - chip) % chips
    behind = (chip - both // 2) % chips
    forward = jnp.where(ahead < half, ahead, -1)
    backward = jnp.where(ahead > half, behind, -1)

    way = jnp.where(backward > 0, blocks + backward // NEAR, forward // NEAR)
    hits = (way[None, :] == numbers(2 * blocks)[:, None]) & (way % blocks > 0)[None, :]
    flag = (jnp.max(jnp.sum(hits.astype(jnp.int32), axis=1)) > PACKED).astype(jnp.int32)

    distance = jnp.where(core == 0, forward, backward)
    block = distance // NEAR
    slot = distance * CELL + crossing * PAIR + source * SLOTS + ranks
    ahead_of = (block[:, None] == block[None, :]) & (slot[None, :] < slot[:, None])
    order = jnp.sum(ahead_of.astype(jnp.int32), axis=1)
    line = jnp.where(block == 0, slot, BLOCK + (block - 1) * PACKED + order)
    line = jnp.where((distance >= 0) & ((block == 0) | (order < PACKED)), line, -1)
    first = BLOCK + (blocks - 1) * PACKED
    opposite = (ahead == half) & (source == 0)
    line = jnp.where(opposite, first + crossing * SLOTS + ranks, line)
    lines = numbers(first + PAIR)
    send_pick = onehot(lines, line)
    noted_slot = jnp.sum(
        jnp.where(lines[:, None] == line[None, :], slot[None, :] % BLOCK + 1, 0), axis=1
    )
    step = blocks * CELL
    side = step // 2

    def relay_row(index, a):
        across = (index // PAIR) % 2
        return (index // CELL) * step + across * side + a * PAIR + index % PAIR

    def flag_in(block):
        return block[0, cut + 1].astype(jnp.int32)

    cut = wide // PARTS
    shares = [slice(h * cut, (h + 1) * cut) for h in range(PARTS)]
    sends, first_leg = [], []
    for h, share in enumerate(shares):
        both_rows = jnp.concatenate([rows[:, share], far_rows[:, share]], axis=0)
        send = picked(send_pick, both_rows)
        sends.append(send)
        came = []
        for a in range(1, blocks):
            part = slice(BLOCK + (a - 1) * PACKED, BLOCK + a * PACKED)
            piece = noted(send[part], noted_slot[part], flag) if h == 0 else send[part]
            came.append(moved(piece, chip_step=a * NEAR))
        first_leg.append(came)
    last = jnp.concatenate([noted(sends[0][first:], numbers(PAIR), flag)]
                           + [send[first:] for send in sends[1:]], axis=1)
    last = moved(last, chip_step=half)
    over = [last[:, : cut + NOTES]]
    over += [last[:, h * cut + NOTES : (h + 1) * cut + NOTES] for h in range(1, PARTS)]

    flags = jnp.maximum(flag, flag_in(over[0]))
    column = [relay_row(numbers(BLOCK), 0)]
    for a, came in enumerate(first_leg[0], 1):
        index = came[:, cut].astype(jnp.int32) - 1
        flags = jnp.maximum(flags, flag_in(came))
        column.append(jnp.where(index < 0, -1, relay_row(index, a)))
    relay_pick = onehot(numbers(NEAR * step), jnp.concatenate(column))
    raised = jnp.where(numbers(cut + NOTES) == cut + 1, flags, 0).astype(jnp.float32)

    products, seen, previous = 0.0, None, []
    for h, share in enumerate(shares):
        own = sends[h][:BLOCK]
        own = noted(own, numbers(BLOCK), flag) if h == 0 else own
        came = first_leg[h]
        if h:
            came, previous = lax.optimization_barrier((came, previous))
        hold = jnp.concatenate([own] + came, axis=0)
        relay = jnp.dot(relay_pick, hold, preferred_element_type=jnp.float32)
        relay = ((relay + raised[None, :]) if h == 0 else relay).astype(jnp.bfloat16)
        arrived = [relay[:step]]
        for b in range(1, NEAR):
            arrived.append(moved(relay[b * step : (b + 1) * step], chip_step=b))
        previous = arrived[1:]
        if h:
            arrived, products = lax.optimization_barrier((arrived, products))
        given = jnp.concatenate([p[side:] for p in arrived] + [over[h][SLOTS:]], axis=0)
        kept = jnp.concatenate([p[:side] for p in arrived] + [over[h][:SLOTS]], axis=0)
        got = moved(given, flip=True)
        if h == 0:
            seen = jnp.maximum(jnp.max(kept[:, cut + 1]), jnp.max(got[:, cut + 1]))
        met = jnp.concatenate([kept[:, :cut], got[:, :cut]], axis=0)
        dims = (((1,), (1,)), ((), ()))
        products += lax.dot_general(
            met, weight[:, share], dims, preferred_element_type=jnp.float32
        )
    products = products.astype(jnp.bfloat16)

    spot = numbers(kept.shape[0])
    main = spot < NEAR * step // 2
    far = jnp.where(main, (spot % (step // 2)) // PAIR * NEAR + spot // (step // 2), half)
    other = jnp.where(main, (spot // SLOTS) % 2, 0)

    def target(lane):
        sign = 1 - 2 * lane
        return (((chip - sign * far) % chips) * 2 + (lane + other) % 2) * SLOTS + spot % SLOTS

    targets = jnp.concatenate([target(core), target(1 - core)])
    places = numbers(experts * SLOTS)
    returned = lax.all_to_all(
        picked(onehot(places, targets), products),
        "expert",
        split_axis=0,
        concat_axis=0,
        tiled=True,
    )
    return picked(onehot(expert * SLOTS + rank, places), returned), seen


def local(cotangent, expert_ids, route_weight, saved_preact, down_weight):
    weight = down_weight[0]
    width = weight.shape[0]
    far_rows = moved(cotangent, flip=True)
    expert = moved(expert_ids[:, 0], section_step=1)
    far_expert = moved(expert_ids[:, 0], section_step=1, flip=True)
    rank = ranked(expert)
    result, full = packed(cotangent, far_rows, expert, far_expert, rank, weight)
    result = lax.cond(
        full > 0,
        lambda: direct(cotangent, expert, rank, weight),
        lambda: result,
    )

    sections = lax.axis_size("section")
    route = [((i + 1) % sections, i) for i in range(sections)]
    back_hidden = lax.ppermute(result, "section", route)
    gate_value = saved_preact[:, :width].astype(jnp.float32)
    up_value = saved_preact[:, width:].astype(jnp.float32)
    sigmoid_gate = jax.nn.sigmoid(gate_value)
    activated = gate_value * sigmoid_gate
    hidden = activated * up_value
    result_float = back_hidden.astype(jnp.float32)
    d_route = jnp.sum(result_float * hidden, axis=1)
    grad_hidden = route_weight[:, None] * result_float
    d_gate = grad_hidden * up_value * sigmoid_gate * (1.0 + gate_value * (1.0 - sigmoid_gate))
    d_up = grad_hidden * activated
    d_preact = jnp.concatenate([d_gate, d_up], axis=1).astype(jnp.bfloat16)
    return (d_preact, d_route)


def solution(mesh):
    in_specs = (
        P(("section", "expert"), None),
        P(("section", "expert"), None),
        P(("section", "expert")),
        P(("section", "expert"), None),
        P("expert", None, None),
    )
    out_specs = (P(("section", "expert"), None), P(("section", "expert")))
    return jax.shard_map(local, mesh=mesh, in_specs=in_specs, out_specs=out_specs, check_vma=False)
```

profile of v0, /device:TPU:6, one launch (start us, length us, event | category | flops | bytes accessed | tf_op | source)
XLA Modules:
  0.0 321.2 jit_solution(5729424487975042924)
XLA Ops:
  0.6 2.8 collective-permute-start.1
  3.5 3.4 %collective-permute-start = (s32[128]{0:T(128)}, s32[128]{0:T(128)S(1)}, u32[]{:S(2)}, u32[]{:S(2)}) collective-permute-start(s32[128]{0:T(128)} %bitcast.22), channel_id=1, source_target_pairs={{0,64},{1,65},{2,66},{3,67},{4,68},{5,69},{6,70},{7,71},{8,72},{9,... | collective-permute-start | bytes 1544 | tf_op jit(solution)/shard_map/ppermute | solution.py:34
  6.9 2.3 collective-permute-start.2
  9.2 1.3 fusion.105
  10.6 0.2 convert_reduce_fusion.1
  10.7 0.2 convert_reduce_fusion.2
  11.0 0.2 convert_reduce_fusion
  11.3 0.1 convert_reduce_fusion.3
  11.4 0.6 reduce_max.27
  12.7 0.1 select_reduce_fusion
  12.9 0.1 select_convert_fusion.1
  13.0 0.1 fusion.106
  13.1 0.4 convolution_convert_fusion.4
  13.6 0.4 convolution_convert_fusion.5
  14.0 0.4 copy-done.1
  14.6 29.0 %collective-permute-start.6 = (bf16[8,4224]{1,0:T(8,128)(2,1)S(1)}, bf16[8,4224]{1,0:T(8,128)(2,1)S(1)}, u32[]{:S(2)}, u32[]{:S(2)}) collective-permute-start(bf16[8,4224]{1,0:T(8,128)(2,1)S(1)} %pad_maximum_fusion.4), channel_id=1, source_target_pairs={{0,32},{1,33},{2,34},{3,35},{4,36},{5,37},{6,38},{7,39},{8,40},{9,... | collective-permute-start | bytes 202760 | tf_op jit(solution)/shard_map/ppermute | solution.py:27
  43.5 7.9 %collective-permute-start.13 = (bf16[48,2048]{1,0:T(8,128)(2,1)S(1)}, bf16[48,2048]{1,0:T(8,128)(2,1)S(1)}, u32[]{:S(2)}, u32[]{:S(2)}) collective-permute-start(bf16[48,2048]{1,0:T(8,128)(2,1)S(1)} %get-tuple-element.53), channel_id=1, source_target_pairs={{0,24},{1,41},{2,26},{3,43},{4,28},{5,45},{6,30},{7,47},{8,32},{9,... | collective-permute-start | bytes 589832 | tf_op jit(solution)/shard_map/ppermute | solution.py:27
  51.5 1.9 collective-permute-start.12
  53.4 3.5 %collective-permute-start.11 = (bf16[48,2048]{1,0:T(8,128)(2,1)S(1)}, bf16[48,2048]{1,0:T(8,128)(2,1)S(1)}, u32[]{:S(2)}, u32[]{:S(2)}) collective-permute-start(bf16[48,2048]{1,0:T(8,128)(2,1)S(1)} %get-tuple-element.55), channel_id=1, source_target_pairs={{0,8},{1,57},{2,10},{3,59},{4,12},{5,61},{6,14},{7,63},{8,16},{9,1... | collective-permute-start | bytes 589832 | tf_op jit(solution)/shard_map/ppermute | solution.py:27
  57.0 9.1 %collective-permute-start.3 = (bf16[48,2176]{1,0:T(8,128)(2,1)S(1)}, bf16[48,2176]{1,0:T(8,128)(2,1)S(1)}, u32[]{:S(2)}, u32[]{:S(2)}) collective-permute-start(bf16[48,2176]{1,0:T(8,128)(2,1)S(1)} %pad_maximum_fusion.1), channel_id=1, source_target_pairs={{0,8},{1,57},{2,10},{3,59},{4,12},{5,61},{6,14},{7,63},{8,16},{9,1... | collective-permute-start | bytes 626696 | tf_op jit(solution)/shard_map/ppermute | solution.py:27
  66.1 10.9 %collective-permute-start.4 = (bf16[48,2176]{1,0:T(8,128)(2,1)S(1)}, bf16[48,2176]{1,0:T(8,128)(2,1)S(1)}, u32[]{:S(2)}, u32[]{:S(2)}) collective-permute-start(bf16[48,2176]{1,0:T(8,128)(2,1)S(1)} %pad_maximum_fusion.2), channel_id=1, source_target_pairs={{0,16},{1,49},{2,18},{3,51},{4,20},{5,53},{6,22},{7,55},{8,24},{9,... | collective-permute-start | bytes 626696 | tf_op jit(solution)/shard_map/ppermute | solution.py:27
  77.1 0.6 slice.257
  78.3 12.5 %collective-permute-done.3 = bf16[48,2176]{1,0:T(8,128)(2,1)S(1)} collective-permute-done((bf16[48,2176]{1,0:T(8,128)(2,1)S(1)}, bf16[48,2176]{1,0:T(8,128)(2,1)S(1)}, u32[]{:S(2)}, u32[]{:S(2)}) %collective-permute-start.3) | collective-permute-done | bytes 208928 | tf_op jit(solution)/shard_map/ppermute | solution.py:27
  90.9 11.5 %collective-permute-start.5 = (bf16[48,2176]{1,0:T(8,128)(2,1)S(1)}, bf16[48,2176]{1,0:T(8,128)(2,1)S(1)}, u32[]{:S(2)}, u32[]{:S(2)}) collective-permute-start(bf16[48,2176]{1,0:T(8,128)(2,1)S(1)} %pad_maximum_fusion.3), channel_id=1, source_target_pairs={{0,24},{1,41},{2,26},{3,43},{4,28},{5,45},{6,30},{7,47},{8,32},{9,... | collective-permute-start | bytes 626696 | tf_op jit(solution)/shard_map/ppermute | solution.py:27
  102.3 0.6 slice.258
  103.6 0.1 add_reduce_fusion.2
  103.7 0.6 slice.259
  105.0 0.1 add_reduce_fusion.1
  105.1 47.2 %collective-permute-done.5 = bf16[48,2176]{1,0:T(8,128)(2,1)S(1)} collective-permute-done((bf16[48,2176]{1,0:T(8,128)(2,1)S(1)}, bf16[48,2176]{1,0:T(8,128)(2,1)S(1)}, u32[]{:S(2)}, u32[]{:S(2)}) %collective-permute-start.5) | collective-permute-done | bytes 208928 | tf_op jit(solution)/shard_map/ppermute | solution.py:27
  152.3 0.6 slice.260
  153.6 0.1 add_reduce_fusion
  153.7 0.1 pad_add_fusion.2
  153.8 0.5 fusion.6
  154.4 18.0 %collective-permute-start.9 = (bf16[64,2176]{1,0:T(8,128)(2,1)S(1)}, bf16[64,2176]{1,0:T(8,128)(2,1)S(1)}, u32[]{:S(2)}, u32[]{:S(2)}) collective-permute-start(bf16[64,2176]{1,0:T(8,128)(2,1)S(1)} %get-tuple-element.42), channel_id=1, source_target_pairs={{0,6},{1,59},{2,8},{3,61},{4,10},{5,63},{6,12},{7,1},{8,14},{9,3},... | collective-permute-start | bytes 835592 | tf_op jit(solution)/shard_map/ppermute | solution.py:27
  172.4 1.9 collective-permute-start.8
  174.4 2.5 collective-permute-start.7
  176.9 5.4 %collective-permute-done.9 = bf16[64,2176]{1,0:T(8,128)(2,1)S(1)} collective-permute-done((bf16[64,2176]{1,0:T(8,128)(2,1)S(1)}, bf16[64,2176]{1,0:T(8,128)(2,1)S(1)}, u32[]{:S(2)}, u32[]{:S(2)}) %collective-permute-start.9) | collective-permute-done | bytes 278560 | tf_op jit(solution)/shard_map/ppermute | solution.py:27
  182.3 3.7 %collective-permute-done.8 = bf16[64,2176]{1,0:T(8,128)(2,1)S(1)} collective-permute-done((bf16[64,2176]{1,0:T(8,128)(2,1)S(1)}, bf16[64,2176]{1,0:T(8,128)(2,1)S(1)}, u32[]{:S(2)}, u32[]{:S(2)}) %collective-permute-start.8) | collective-permute-done | bytes 278560 | tf_op jit(solution)/shard_map/ppermute | solution.py:27
  186.0 2.3 collective-permute-done.7
  188.5 2.2 collective-permute-start.10
  190.7 0.4 convolution_convert_fusion.3
  191.2 6.1 %collective-permute-start.16 = (bf16[64,2048]{1,0:T(8,128)(2,1)S(1)}, bf16[64,2048]{1,0:T(8,128)(2,1)S(1)}, u32[]{:S(2)}, u32[]{:S(2)}) collective-permute-start(bf16[64,2048]{1,0:T(8,128)(2,1)S(1)} %get-tuple-element.45), channel_id=1, source_target_pairs={{0,6},{1,59},{2,8},{3,61},{4,10},{5,63},{6,12},{7,1},{8,14},{9,3},... | collective-permute-start | bytes 786440 | tf_op jit(solution)/shard_map/ppermute | solution.py:27
  197.3 3.9 %collective-permute-start.15 = (bf16[64,2048]{1,0:T(8,128)(2,1)S(1)}, bf16[64,2048]{1,0:T(8,128)(2,1)S(1)}, u32[]{:S(2)}, u32[]{:S(2)}) collective-permute-start(bf16[64,2048]{1,0:T(8,128)(2,1)S(1)} %get-tuple-element.46), channel_id=1, source_target_pairs={{0,4},{1,61},{2,6},{3,63},{4,8},{5,1},{6,10},{7,3},{8,12},{9,5},{1... | collective-permute-start | bytes 786440 | tf_op jit(solution)/shard_map/ppermute | solution.py:27
  201.2 4.9 %collective-permute-start.14 = (bf16[64,2048]{1,0:T(8,128)(2,1)S(1)}, bf16[64,2048]{1,0:T(8,128)(2,1)S(1)}, u32[]{:S(2)}, u32[]{:S(2)}) collective-permute-start(bf16[64,2048]{1,0:T(8,128)(2,1)S(1)} %get-tuple-element.47), channel_id=1, source_target_pairs={{0,2},{1,63},{2,4},{3,1},{4,6},{5,3},{6,8},{7,5},{8,10},{9,7},{10,... | collective-permute-start | bytes 786440 | tf_op jit(solution)/shard_map/ppermute | solution.py:27
  206.1 0.8 copy-done.2
  207.0 2.3 fusion.4
  209.4 2.8 collective-permute-done.15
  212.1 4.4 %collective-permute-done.14 = bf16[64,2048]{1,0:T(8,128)(2,1)S(1)} collective-permute-done((bf16[64,2048]{1,0:T(8,128)(2,1)S(1)}, bf16[64,2048]{1,0:T(8,128)(2,1)S(1)}, u32[]{:S(2)}, u32[]{:S(2)}) %collective-permute-start.14) | collective-permute-done | bytes 262176 | tf_op jit(solution)/shard_map/ppermute | solution.py:27
  216.7 1.9 collective-permute-start.17
  218.7 1.8 collective-permute-done.17
  220.5 0.9 concatenate.182
  221.4 4.9 %convolution_convert_fusion.6 = bf16[256,1024]{1,0:T(8,128)(2,1)} fusion(f32[264,1024]{1,0:T(8,128)} %fusion.4, bf16[264,2048]{1,0:T(8,128)(2,1)S(1)} %concatenate.182, bf16[1024,4096]{1,0:T(8,128)(2,1)} %bitcast.16, s32[264]{0:T(512)S(1)} %pad_add_fusion), kind=kOutput, calls=%fused_computation.17 | convolution fusion | flops 1246578688 | bytes 6882336 | tf_op jit(solution)/shard_map/dot_general | solution.py:46
  226.3 2.1 all_to_all.24
  228.4 13.1 %all-to-all-start.2 = ((bf16[64,4,1024]{2,1,0:T(4,128)(2,1)}), bf16[64,4,1024]{2,1,0:T(4,128)(2,1)S(1)}, u32[]{:S(2)}, u32[]{:S(2)}) async-start(bf16[64,4,1024]{2,1,0:T(4,128)(2,1)} %all_to_all.24), calls=%async_computation.2 | async-start | bytes 1048576 | tf_op jit(solution)/shard_map/all_to_all | solution.py:194
  241.5 0.7 slice_reduce_fusion.1
  242.2 1.5 slice_reduce_fusion
  245.0 62.3 %all-to-all-done.2 = bf16[64,4,1024]{2,1,0:T(4,128)(2,1)S(1)} async-done(((bf16[64,4,1024]{2,1,0:T(4,128)(2,1)}), bf16[64,4,1024]{2,1,0:T(4,128)(2,1)S(1)}, u32[]{:S(2)}, u32[]{:S(2)}) %all-to-all-start.2) | async-done | bytes 524320 | tf_op jit(solution)/shard_map/all_to_all | solution.py:194
  307.3 0.1 all_to_all.26
  307.4 0.3 convolution_convert_fusion.7
  307.7 0.2 conditional.1
  307.9 2.4 collective-permute-start.18
  310.3 8.1 %collective-permute-done.18 = bf16[128,1024]{1,0:T(8,128)(2,1)S(1)} collective-permute-done((bf16[128,1024]{1,0:T(8,128)(2,1)S(1)}, bf16[128,1024]{1,0:T(8,128)(2,1)S(1)}, u32[]{:S(2)}, u32[]{:S(2)}) %collective-permute-start.18) | collective-permute-done | bytes 262176 | tf_op jit(solution)/shard_map/ppermute | solution.py:220
  318.4 2.0 fusion.41
  320.4 0.8 pad_maximum_fusion
  (65 shorter events, 1.1 us)
Async XLA Ops:
  0.6 9.9 %collective-permute-start.1 = (s32[128]{0:T(128)}, s32[128]{0:T(128)S(1)}, u32[]{:S(2)}, u32[]{:S(2)}) collective-permute-start(s32[128]{0:T(128)} %bitcast.21), channel_id=1, source_target_pairs={{0,65},{1,64},{2,67},{3,66},{4,69},{5,68},{6,71},{7,70},{8,73},{9,... | collective-permute-start | bytes 1544 | tf_op jit(solution)/shard_map/ppermute | solution.py:34
  3.5 7.3 %collective-permute-start = (s32[128]{0:T(128)}, s32[128]{0:T(128)S(1)}, u32[]{:S(2)}, u32[]{:S(2)}) collective-permute-start(s32[128]{0:T(128)} %bitcast.22), channel_id=1, source_target_pairs={{0,64},{1,65},{2,66},{3,67},{4,68},{5,69},{6,70},{7,71},{8,72},{9,... | collective-permute-start | bytes 1544 | tf_op jit(solution)/shard_map/ppermute | solution.py:34
  6.9 6.1 %collective-permute-start.2 = (bf16[128,4096]{1,0:T(8,128)(2,1)}, bf16[128,4096]{1,0:T(8,128)(2,1)S(1)}, u32[]{:S(2)}, u32[]{:S(2)}) collective-permute-start(bf16[128,4096]{1,0:T(8,128)(2,1)} %param.7), channel_id=1, source_target_pairs={{0,1},{1,0},{2,3},{3,2},{4,5},{5,4},{6,7},{7,6},{8,9},{9,8},{10,11... | collective-permute-start | bytes 3145736 | tf_op jit(solution)/shard_map/ppermute | solution.py:27
  13.5 0.9 copy-start.1
  14.6 51.6 %collective-permute-start.6 = (bf16[8,4224]{1,0:T(8,128)(2,1)S(1)}, bf16[8,4224]{1,0:T(8,128)(2,1)S(1)}, u32[]{:S(2)}, u32[]{:S(2)}) collective-permute-start(bf16[8,4224]{1,0:T(8,128)(2,1)S(1)} %pad_maximum_fusion.4), channel_id=1, source_target_pairs={{0,32},{1,33},{2,34},{3,35},{4,36},{5,37},{6,38},{7,39},{8,40},{9,... | collective-permute-start | bytes 202760 | tf_op jit(solution)/shard_map/ppermute | solution.py:27
  43.5 130.8 %collective-permute-start.13 = (bf16[48,2048]{1,0:T(8,128)(2,1)S(1)}, bf16[48,2048]{1,0:T(8,128)(2,1)S(1)}, u32[]{:S(2)}, u32[]{:S(2)}) collective-permute-start(bf16[48,2048]{1,0:T(8,128)(2,1)S(1)} %get-tuple-element.53), channel_id=1, source_target_pairs={{0,24},{1,41},{2,26},{3,43},{4,28},{5,45},{6,30},{7,47},{8,32},{9,... | collective-permute-start | bytes 589832 | tf_op jit(solution)/shard_map/ppermute | solution.py:27
  51.5 125.4 %collective-permute-start.12 = (bf16[48,2048]{1,0:T(8,128)(2,1)S(1)}, bf16[48,2048]{1,0:T(8,128)(2,1)S(1)}, u32[]{:S(2)}, u32[]{:S(2)}) collective-permute-start(bf16[48,2048]{1,0:T(8,128)(2,1)S(1)} %get-tuple-element.54), channel_id=1, source_target_pairs={{0,16},{1,49},{2,18},{3,51},{4,20},{5,53},{6,22},{7,55},{8,24},{9,... | collective-permute-start | bytes 589832 | tf_op jit(solution)/shard_map/ppermute | solution.py:27
  53.4 123.5 %collective-permute-start.11 = (bf16[48,2048]{1,0:T(8,128)(2,1)S(1)}, bf16[48,2048]{1,0:T(8,128)(2,1)S(1)}, u32[]{:S(2)}, u32[]{:S(2)}) collective-permute-start(bf16[48,2048]{1,0:T(8,128)(2,1)S(1)} %get-tuple-element.55), channel_id=1, source_target_pairs={{0,8},{1,57},{2,10},{3,59},{4,12},{5,61},{6,14},{7,63},{8,16},{9,1... | collective-permute-start | bytes 589832 | tf_op jit(solution)/shard_map/ppermute | solution.py:27
  57.0 33.9 %collective-permute-start.3 = (bf16[48,2176]{1,0:T(8,128)(2,1)S(1)}, bf16[48,2176]{1,0:T(8,128)(2,1)S(1)}, u32[]{:S(2)}, u32[]{:S(2)}) collective-permute-start(bf16[48,2176]{1,0:T(8,128)(2,1)S(1)} %pad_maximum_fusion.1), channel_id=1, source_target_pairs={{0,8},{1,57},{2,10},{3,59},{4,12},{5,61},{6,14},{7,63},{8,16},{9,1... | collective-permute-start | bytes 626696 | tf_op jit(solution)/shard_map/ppermute | solution.py:27
  66.1 37.6 %collective-permute-start.4 = (bf16[48,2176]{1,0:T(8,128)(2,1)S(1)}, bf16[48,2176]{1,0:T(8,128)(2,1)S(1)}, u32[]{:S(2)}, u32[]{:S(2)}) collective-permute-start(bf16[48,2176]{1,0:T(8,128)(2,1)S(1)} %pad_maximum_fusion.2), channel_id=1, source_target_pairs={{0,16},{1,49},{2,18},{3,51},{4,20},{5,53},{6,22},{7,55},{8,24},{9,... | collective-permute-start | bytes 626696 | tf_op jit(solution)/shard_map/ppermute | solution.py:27
  90.9 61.5 %collective-permute-start.5 = (bf16[48,2176]{1,0:T(8,128)(2,1)S(1)}, bf16[48,2176]{1,0:T(8,128)(2,1)S(1)}, u32[]{:S(2)}, u32[]{:S(2)}) collective-permute-start(bf16[48,2176]{1,0:T(8,128)(2,1)S(1)} %pad_maximum_fusion.3), channel_id=1, source_target_pairs={{0,24},{1,41},{2,26},{3,43},{4,28},{5,45},{6,30},{7,47},{8,32},{9,... | collective-permute-start | bytes 626696 | tf_op jit(solution)/shard_map/ppermute | solution.py:27
  153.8 53.2 %slice-start.1 = ((s8[8388608]{0:T(1024)(128)(4,1)}), s8[4194304]{0:T(1024)(128)(4,1)S(1)}, s32[]{:S(2)}) async-start(s8[8388608]{0:T(1024)(128)(4,1)} %bitcast.18), calls=%async_computation.4 | async-start | bytes 8388608
  154.3 36.4 %slice-start = ((bf16[216,2048]{1,0:T(8,128)(2,1)}), bf16[64,2048]{1,0:T(8,128)(2,1)S(1)}, s32[]{:S(2)}) async-start(bf16[216,2048]{1,0:T(8,128)(2,1)} %copy-done.1), calls=%async_computation.3 | async-start | bytes 524288 | tf_op jit(solution)/shard_map/slice | solution.py:157
  154.4 27.9 %collective-permute-start.9 = (bf16[64,2176]{1,0:T(8,128)(2,1)S(1)}, bf16[64,2176]{1,0:T(8,128)(2,1)S(1)}, u32[]{:S(2)}, u32[]{:S(2)}) collective-permute-start(bf16[64,2176]{1,0:T(8,128)(2,1)S(1)} %get-tuple-element.42), channel_id=1, source_target_pairs={{0,6},{1,59},{2,8},{3,61},{4,10},{5,63},{6,12},{7,1},{8,14},{9,3},... | collective-permute-start | bytes 835592 | tf_op jit(solution)/shard_map/ppermute | solution.py:27
  172.4 13.5 %collective-permute-start.8 = (bf16[64,2176]{1,0:T(8,128)(2,1)S(1)}, bf16[64,2176]{1,0:T(8,128)(2,1)S(1)}, u32[]{:S(2)}, u32[]{:S(2)}) collective-permute-start(bf16[64,2176]{1,0:T(8,128)(2,1)S(1)} %get-tuple-element.43), channel_id=1, source_target_pairs={{0,4},{1,61},{2,6},{3,63},{4,8},{5,1},{6,10},{7,3},{8,12},{9,5},{1... | collective-permute-start | bytes 835592 | tf_op jit(solution)/shard_map/ppermute | solution.py:27
  174.4 13.9 %collective-permute-start.7 = (bf16[64,2176]{1,0:T(8,128)(2,1)S(1)}, bf16[64,2176]{1,0:T(8,128)(2,1)S(1)}, u32[]{:S(2)}, u32[]{:S(2)}) collective-permute-start(bf16[64,2176]{1,0:T(8,128)(2,1)S(1)} %get-tuple-element.44), channel_id=1, source_target_pairs={{0,2},{1,63},{2,4},{3,1},{4,6},{5,3},{6,8},{7,5},{8,10},{9,7},{10,... | collective-permute-start | bytes 835592 | tf_op jit(solution)/shard_map/ppermute | solution.py:27
  188.4 18.6 %slice-start.2 = ((s8[8388608]{0:T(1024)(128)(4,1)}), s8[4194304]{0:T(1024)(128)(4,1)S(1)}, s32[]{:S(2)}) async-start(s8[8388608]{0:T(1024)(128)(4,1)} %bitcast.18), calls=%async_computation.5 | async-start | bytes 8388608
  188.5 17.6 %collective-permute-start.10 = (bf16[132,2176]{1,0:T(8,128)(2,1)S(1)}, bf16[132,2176]{1,0:T(8,128)(2,1)S(1)}, u32[]{:S(2)}, u32[]{:S(2)}) collective-permute-start(bf16[132,2176]{1,0:T(8,128)(2,1)S(1)} %get-tuple-element.78), channel_id=1, source_target_pairs={{0,1},{1,0},{2,3},{3,2},{4,5},{5,4},{6,7},{7,6},{8,9},{9,8},{10,11... | collective-permute-start | bytes 1723400 | tf_op jit(solution)/shard_map/ppermute | solution.py:27
  191.2 18.2 %collective-permute-start.16 = (bf16[64,2048]{1,0:T(8,128)(2,1)S(1)}, bf16[64,2048]{1,0:T(8,128)(2,1)S(1)}, u32[]{:S(2)}, u32[]{:S(2)}) collective-permute-start(bf16[64,2048]{1,0:T(8,128)(2,1)S(1)} %get-tuple-element.45), channel_id=1, source_target_pairs={{0,6},{1,59},{2,8},{3,61},{4,10},{5,63},{6,12},{7,1},{8,14},{9,3},... | collective-permute-start | bytes 786440 | tf_op jit(solution)/shard_map/ppermute | solution.py:27
  197.3 14.8 %collective-permute-start.15 = (bf16[64,2048]{1,0:T(8,128)(2,1)S(1)}, bf16[64,2048]{1,0:T(8,128)(2,1)S(1)}, u32[]{:S(2)}, u32[]{:S(2)}) collective-permute-start(bf16[64,2048]{1,0:T(8,128)(2,1)S(1)} %get-tuple-element.46), channel_id=1, source_target_pairs={{0,4},{1,61},{2,6},{3,63},{4,8},{5,1},{6,10},{7,3},{8,12},{9,5},{1... | collective-permute-start | bytes 786440 | tf_op jit(solution)/shard_map/ppermute | solution.py:27
  201.2 15.4 %collective-permute-start.14 = (bf16[64,2048]{1,0:T(8,128)(2,1)S(1)}, bf16[64,2048]{1,0:T(8,128)(2,1)S(1)}, u32[]{:S(2)}, u32[]{:S(2)}) collective-permute-start(bf16[64,2048]{1,0:T(8,128)(2,1)S(1)} %get-tuple-element.47), channel_id=1, source_target_pairs={{0,2},{1,63},{2,4},{3,1},{4,6},{5,3},{6,8},{7,5},{8,10},{9,7},{10,... | collective-permute-start | bytes 786440 | tf_op jit(solution)/shard_map/ppermute | solution.py:27
  206.1 0.8 copy-start.2
  216.7 3.9 %collective-permute-start.17 = (bf16[132,2048]{1,0:T(8,128)(2,1)S(1)}, bf16[132,2048]{1,0:T(8,128)(2,1)S(1)}, u32[]{:S(2)}, u32[]{:S(2)}) collective-permute-start(bf16[132,2048]{1,0:T(8,128)(2,1)S(1)} %get-tuple-element.76), channel_id=1, source_target_pairs={{0,1},{1,0},{2,3},{3,2},{4,5},{5,4},{6,7},{7,6},{8,9},{9,8},{10,11... | collective-permute-start | bytes 1622024 | tf_op jit(solution)/shard_map/ppermute | solution.py:27
  226.3 81.1 %copy-start = (bf16[128,4096]{1,0:T(8,128)(2,1)S(1)}, bf16[128,4096]{1,0:T(8,128)(2,1)}, u32[]{:S(2)}) copy-start(bf16[128,4096]{1,0:T(8,128)(2,1)} %param.7) | copy-start | bytes 3145732
  228.4 78.9 %all-to-all-start.2 = ((bf16[64,4,1024]{2,1,0:T(4,128)(2,1)}), bf16[64,4,1024]{2,1,0:T(4,128)(2,1)S(1)}, u32[]{:S(2)}, u32[]{:S(2)}) async-start(bf16[64,4,1024]{2,1,0:T(4,128)(2,1)} %all_to_all.24), calls=%async_computation.2 | async-start | bytes 1048576 | tf_op jit(solution)/shard_map/all_to_all | solution.py:194
  307.7 10.7 %copy-start.3 = (f32[128]{0:T(128)S(1)}, f32[128]{0:T(128)}, u32[]{:S(2)}) copy-start(f32[128]{0:T(128)} %param.9) | copy-start | bytes 1540
  307.9 10.5 %collective-permute-start.18 = (bf16[128,1024]{1,0:T(8,128)(2,1)S(1)}, bf16[128,1024]{1,0:T(8,128)(2,1)S(1)}, u32[]{:S(2)}, u32[]{:S(2)}) collective-permute-start(bf16[128,1024]{1,0:T(8,128)(2,1)S(1)} %get-tuple-element.90), channel_id=1, source_target_pairs={{64,0},{128,64},{192,128},{256,192},{320,256},{384,320},{448,384},... | collective-permute-start | bytes 786440 | tf_op jit(solution)/shard_map/ppermute | solution.py:220
where the time goes:
time: 322 us; the launch traced here: 321 us
  waiting for transfers between devices  150 us (47%)
  starting transfers between devices  139 us (43%)
  matrix products  9.24 us (3%)
  local copies, waits for them, and re-layouts  8.77 us (3%)
  other arithmetic  7.29 us (2%)
  between operations  5.94 us (2%)
    ppermute x16, starting transfers between devices, moved(): lax.ppermute(block, 'expert', [(i, target(i)) for i in range(experts)])  118 us
    ppermute x16, waiting for transfers between devices, moved(): lax.ppermute(block, 'expert', [(i, target(i)) for i in range(experts)])  80.2 us
    all_to_all x1, waiting for transfers between devices, packed(): lax.all_to_all(picked(onehot(places, targets), products), 'expert', split...  62.3 us
    all_to_all x1, starting transfers between devices, packed(): lax.all_to_all(picked(onehot(places, targets), products), 'expert', split...  13.1 us
    ppermute x1, waiting for transfers between devices, local(): back_hidden = lax.ppermute(result, 'section', route)  8.06 us
  transfers between devices with their start and end apart: 20, of which 10 were waited for; matrix products, arithmetic and copies ran while one was open for 4% of the time, Pallas kernels for 0%

commit v1 on v0

--- a/solution.py
+++ b/solution.py
@@ -120,9 +120,6 @@
     def relay_row(index, a):
         across = (index // PAIR) % 2
         return (index // CELL) * step + across * side + a * PAIR + index % PAIR
-
-    def flag_in(block):
-        return block[0, cut + 1].astype(jnp.int32)
 
     cut = wide // PARTS
     shares = [slice(h * cut, (h + 1) * cut) for h in range(PARTS)]
@@ -143,14 +140,11 @@
     over = [last[:, : cut + NOTES]]
     over += [last[:, h * cut + NOTES : (h + 1) * cut + NOTES] for h in range(1, PARTS)]
 
-    flags = jnp.maximum(flag, flag_in(over[0]))
     column = [relay_row(numbers(BLOCK), 0)]
     for a, came in enumerate(first_leg[0], 1):
         index = came[:, cut].astype(jnp.int32) - 1
-        flags = jnp.maximum(flags, flag_in(came))
         column.append(jnp.where(index < 0, -1, relay_row(index, a)))
     relay_pick = onehot(numbers(NEAR * step), jnp.concatenate(column))
-    raised = jnp.where(numbers(cut + NOTES) == cut + 1, flags, 0).astype(jnp.float32)
 
     products, seen, previous = 0.0, None, []
     for h, share in enumerate(shares):
@@ -161,7 +155,11 @@
             came, previous = lax.optimization_barrier((came, previous))
         hold = jnp.concatenate([own] + came, axis=0)
         relay = jnp.dot(relay_pick, hold, preferred_element_type=jnp.float32)
-        relay = ((relay + raised[None, :]) if h == 0 else relay).astype(jnp.bfloat16)
+        if h == 0:
+            notes = jnp.sum(hold[:, cut:].astype(jnp.float32), axis=0)
+            raised = jnp.where(numbers(NOTES) == 1, jnp.minimum(notes, 1.0), 0.0)
+            relay = relay + jnp.pad(raised, (cut, 0))[None, :]
+        relay = relay.astype(jnp.bfloat16)
         arrived = [relay[:step]]
         for b in range(1, NEAR):
             arrived.append(moved(relay[b * step : (b + 1) * step], chip_step=b))

time: 322 us -> 324 us (level)
  the two profiles are of different devices: /device:TPU:6 before, /device:TPU:14 now
where the time goes in v1:
time: 324 us; the launch traced here: 323 us
  starting transfers between devices  172 us (53%)
  waiting for transfers between devices  125 us (39%)
  matrix products  9.23 us (3%)
  other arithmetic  7.33 us (2%)
  local copies, waits for them, and re-layouts  6.01 us (2%)
  between operations  3.3 us (1%)
    ppermute x16, starting transfers between devices, moved(): lax.ppermute(block, 'expert', [(i, target(i)) for i in range(experts)])  150 us
    all_to_all x1, waiting for transfers between devices, packed(): lax.all_to_all(picked(onehot(places, targets), products), 'expert', split...  62.3 us
    ppermute x16, waiting for transfers between devices, moved(): lax.ppermute(block, 'expert', [(i, target(i)) for i in range(experts)])  54.7 us
    all_to_all x1, starting transfers between devices, packed(): lax.all_to_all(picked(onehot(places, targets), products), 'expert', split...  13.3 us
    ppermute x1, waiting for transfers between devices, local(): back_hidden = lax.ppermute(result, 'section', route)  8.12 us
  transfers between devices with their start and end apart: 20, of which 9 were waited for; matrix products, arithmetic and copies ran while one was open for 3% of the time, Pallas kernels for 0%

profile of v1, /device:TPU:14, one launch (start us, length us, event | category | flops | bytes accessed | tf_op | source)
XLA Modules:
  0.0 323.2 jit_solution(1166562804391916734)
XLA Ops:
  0.6 2.8 collective-permute-start.1
  3.5 3.4 %collective-permute-start = (s32[128]{0:T(128)}, s32[128]{0:T(128)S(1)}, u32[]{:S(2)}, u32[]{:S(2)}) collective-permute-start(s32[128]{0:T(128)} %bitcast.14), channel_id=1, source_target_pairs={{0,64},{1,65},{2,66},{3,67},{4,68},{5,69},{6,70},{7,71},{8,72},{9,... | collective-permute-start | bytes 1544 | tf_op jit(solution)/shard_map/ppermute | solution.py:34
  6.9 2.3 collective-permute-start.2
  9.2 1.3 fusion.105
  10.6 0.2 convert_reduce_fusion.3
  10.8 0.1 convert_reduce_fusion.4
  10.9 0.6 reduce_max.27
  12.2 0.2 convert_reduce_fusion.2
  12.4 0.2 convert_reduce_fusion
  12.7 0.1 select_reduce_fusion
  12.8 0.1 fusion.109
  12.9 0.1 select_convert_fusion.3
  13.0 0.1 fusion.106
  13.1 0.4 convolution_convert_fusion.5
  13.6 0.4 convolution_convert_fusion.4
  14.1 29.0 %collective-permute-start.9 = (bf16[8,4224]{1,0:T(8,128)(2,1)S(1)}, bf16[8,4224]{1,0:T(8,128)(2,1)S(1)}, u32[]{:S(2)}, u32[]{:S(2)}) collective-permute-start(bf16[8,4224]{1,0:T(8,128)(2,1)S(1)} %pad_maximum_fusion.4), channel_id=1, source_target_pairs={{0,32},{1,33},{2,34},{3,35},{4,36},{5,37},{6,38},{7,39},{8,40},{9,... | collective-permute-start | bytes 202760 | tf_op jit(solution)/shard_map/ppermute | solution.py:27
  43.1 6.1 %collective-permute-start.4 = (bf16[48,2176]{1,0:T(8,128)(2,1)S(1)}, bf16[48,2176]{1,0:T(8,128)(2,1)S(1)}, u32[]{:S(2)}, u32[]{:S(2)}) collective-permute-start(bf16[48,2176]{1,0:T(8,128)(2,1)S(1)} %pad_maximum_fusion.2), channel_id=1, source_target_pairs={{0,16},{1,49},{2,18},{3,51},{4,20},{5,53},{6,22},{7,55},{8,24},{9,... | collective-permute-start | bytes 626696 | tf_op jit(solution)/shard_map/ppermute | solution.py:27
  49.3 3.7 %collective-permute-start.5 = (bf16[48,2176]{1,0:T(8,128)(2,1)S(1)}, bf16[48,2176]{1,0:T(8,128)(2,1)S(1)}, u32[]{:S(2)}, u32[]{:S(2)}) collective-permute-start(bf16[48,2176]{1,0:T(8,128)(2,1)S(1)} %pad_maximum_fusion.3), channel_id=1, source_target_pairs={{0,24},{1,41},{2,26},{3,43},{4,28},{5,45},{6,30},{7,47},{8,32},{9,... | collective-permute-start | bytes 626696 | tf_op jit(solution)/shard_map/ppermute | solution.py:27
  53.1 3.5 %collective-permute-start.3 = (bf16[48,2176]{1,0:T(8,128)(2,1)S(1)}, bf16[48,2176]{1,0:T(8,128)(2,1)S(1)}, u32[]{:S(2)}, u32[]{:S(2)}) collective-permute-start(bf16[48,2176]{1,0:T(8,128)(2,1)S(1)} %pad_maximum_fusion.1), channel_id=1, source_target_pairs={{0,8},{1,57},{2,10},{3,59},{4,12},{5,61},{6,14},{7,63},{8,16},{9,1... | collective-permute-start | bytes 626696 | tf_op jit(solution)/shard_map/ppermute | solution.py:27
  56.6 17.5 %collective-permute-start.13 = (bf16[48,2048]{1,0:T(8,128)(2,1)S(1)}, bf16[48,2048]{1,0:T(8,128)(2,1)S(1)}, u32[]{:S(2)}, u32[]{:S(2)}) collective-permute-start(bf16[48,2048]{1,0:T(8,128)(2,1)S(1)} %get-tuple-element.53), channel_id=1, source_target_pairs={{0,24},{1,41},{2,26},{3,43},{4,28},{5,45},{6,30},{7,47},{8,32},{9,... | collective-permute-start | bytes 589832 | tf_op jit(solution)/shard_map/ppermute | solution.py:27
  74.2 6.1 %collective-permute-start.12 = (bf16[48,2048]{1,0:T(8,128)(2,1)S(1)}, bf16[48,2048]{1,0:T(8,128)(2,1)S(1)}, u32[]{:S(2)}, u32[]{:S(2)}) collective-permute-start(bf16[48,2048]{1,0:T(8,128)(2,1)S(1)} %get-tuple-element.54), channel_id=1, source_target_pairs={{0,16},{1,49},{2,18},{3,51},{4,20},{5,53},{6,22},{7,55},{8,24},{9,... | collective-permute-start | bytes 589832 | tf_op jit(solution)/shard_map/ppermute | solution.py:27
  80.3 0.1 add_reduce_fusion.1
  80.4 6.0 %collective-permute-start.11 = (bf16[48,2048]{1,0:T(8,128)(2,1)S(1)}, bf16[48,2048]{1,0:T(8,128)(2,1)S(1)}, u32[]{:S(2)}, u32[]{:S(2)}) collective-permute-start(bf16[48,2048]{1,0:T(8,128)(2,1)S(1)} %get-tuple-element.55), channel_id=1, source_target_pairs={{0,8},{1,57},{2,10},{3,59},{4,12},{5,61},{6,14},{7,63},{8,16},{9,1... | collective-permute-start | bytes 589832 | tf_op jit(solution)/shard_map/ppermute | solution.py:27
  86.5 0.1 add_reduce_fusion
  86.7 0.1 add_reduce_fusion.2
  86.8 0.1 pad_add_fusion.2
  86.9 0.5 fusion.6
  87.4 0.1 fusion.103
  87.5 50.8 %collective-permute-start.6 = (bf16[64,2176]{1,0:T(8,128)(2,1)S(1)}, bf16[64,2176]{1,0:T(8,128)(2,1)S(1)}, u32[]{:S(2)}, u32[]{:S(2)}) collective-permute-start(bf16[64,2176]{1,0:T(8,128)(2,1)S(1)} %get-tuple-element.44), channel_id=1, source_target_pairs={{0,2},{1,63},{2,4},{3,1},{4,6},{5,3},{6,8},{7,5},{8,10},{9,7},{10,... | collective-permute-start | bytes 835592 | tf_op jit(solution)/shard_map/ppermute | solution.py:27
  138.4 22.2 %collective-permute-done.6 = bf16[64,2176]{1,0:T(8,128)(2,1)S(1)} collective-permute-done((bf16[64,2176]{1,0:T(8,128)(2,1)S(1)}, bf16[64,2176]{1,0:T(8,128)(2,1)S(1)}, u32[]{:S(2)}, u32[]{:S(2)}) %collective-permute-start.6) | collective-permute-done | bytes 278560 | tf_op jit(solution)/shard_map/ppermute | solution.py:27
  160.6 2.9 collective-permute-start.7
  163.5 7.7 %collective-permute-done.7 = bf16[64,2176]{1,0:T(8,128)(2,1)S(1)} collective-permute-done((bf16[64,2176]{1,0:T(8,128)(2,1)S(1)}, bf16[64,2176]{1,0:T(8,128)(2,1)S(1)}, u32[]{:S(2)}, u32[]{:S(2)}) %collective-permute-start.7) | collective-permute-done | bytes 278560 | tf_op jit(solution)/shard_map/ppermute | solution.py:27
  171.2 5.5 %collective-permute-start.8 = (bf16[64,2176]{1,0:T(8,128)(2,1)S(1)}, bf16[64,2176]{1,0:T(8,128)(2,1)S(1)}, u32[]{:S(2)}, u32[]{:S(2)}) collective-permute-start(bf16[64,2176]{1,0:T(8,128)(2,1)S(1)} %get-tuple-element.42), channel_id=1, source_target_pairs={{0,6},{1,59},{2,8},{3,61},{4,10},{5,63},{6,12},{7,1},{8,14},{9,3},... | collective-permute-start | bytes 835592 | tf_op jit(solution)/shard_map/ppermute | solution.py:27
  176.7 14.1 %collective-permute-done.8 = bf16[64,2176]{1,0:T(8,128)(2,1)S(1)} collective-permute-done((bf16[64,2176]{1,0:T(8,128)(2,1)S(1)}, bf16[64,2176]{1,0:T(8,128)(2,1)S(1)}, u32[]{:S(2)}, u32[]{:S(2)}) %collective-permute-start.8) | collective-permute-done | bytes 278560 | tf_op jit(solution)/shard_map/ppermute | solution.py:27
  190.9 2.2 collective-permute-start.10
  193.1 0.4 convolution_convert_fusion.3
  193.6 0.1 fusion.104
  193.6 2.6 collective-permute-start.16
  196.2 3.4 %collective-permute-start.15 = (bf16[64,2048]{1,0:T(8,128)(2,1)S(1)}, bf16[64,2048]{1,0:T(8,128)(2,1)S(1)}, u32[]{:S(2)}, u32[]{:S(2)}) collective-permute-start(bf16[64,2048]{1,0:T(8,128)(2,1)S(1)} %get-tuple-element.46), channel_id=1, source_target_pairs={{0,4},{1,61},{2,6},{3,63},{4,8},{5,1},{6,10},{7,3},{8,12},{9,5},{1... | collective-permute-start | bytes 786440 | tf_op jit(solution)/shard_map/ppermute | solution.py:27
  199.6 6.5 %collective-permute-start.14 = (bf16[64,2048]{1,0:T(8,128)(2,1)S(1)}, bf16[64,2048]{1,0:T(8,128)(2,1)S(1)}, u32[]{:S(2)}, u32[]{:S(2)}) collective-permute-start(bf16[64,2048]{1,0:T(8,128)(2,1)S(1)} %get-tuple-element.47), channel_id=1, source_target_pairs={{0,2},{1,63},{2,4},{3,1},{4,6},{5,3},{6,8},{7,5},{8,10},{9,7},{10,... | collective-permute-start | bytes 786440 | tf_op jit(solution)/shard_map/ppermute | solution.py:27
  206.1 0.1 slice.267
  206.2 0.8 copy-done.2
  207.1 2.3 fusion.4
  209.5 2.7 collective-permute-done.16
  212.2 2.6 collective-permute-done.15
  214.8 3.5 %collective-permute-done.14 = bf16[64,2048]{1,0:T(8,128)(2,1)S(1)} collective-permute-done((bf16[64,2048]{1,0:T(8,128)(2,1)S(1)}, bf16[64,2048]{1,0:T(8,128)(2,1)S(1)}, u32[]{:S(2)}, u32[]{:S(2)}) %collective-permute-start.14) | collective-permute-done | bytes 262176 | tf_op jit(solution)/shard_map/ppermute | solution.py:27
  218.5 1.9 collective-permute-start.17
  220.4 0.1 pad_add_fusion
  220.5 1.8 collective-permute-done.17
  222.3 0.9 concatenate.182
  223.2 4.9 %convolution_convert_fusion.6 = bf16[256,1024]{1,0:T(8,128)(2,1)} fusion(f32[264,1024]{1,0:T(8,128)} %fusion.4, bf16[264,2048]{1,0:T(8,128)(2,1)S(1)} %concatenate.182, bf16[1024,4096]{1,0:T(8,128)(2,1)} %bitcast.8, s32[264]{0:T(512)S(1)} %pad_add_fusion), kind=kOutput, calls=%fused_computation.17 | convolution fusion | flops 1246578688 | bytes 6882336 | tf_op jit(solution)/shard_map/dot_general | solution.py:46
  228.1 2.1 all_to_all.24
  230.2 13.3 %all-to-all-start.2 = ((bf16[64,4,1024]{2,1,0:T(4,128)(2,1)}), bf16[64,4,1024]{2,1,0:T(4,128)(2,1)S(1)}, u32[]{:S(2)}, u32[]{:S(2)}) async-start(bf16[64,4,1024]{2,1,0:T(4,128)(2,1)} %all_to_all.24), calls=%async_computation.2 | async-start | bytes 1048576 | tf_op jit(solution)/shard_map/all_to_all | solution.py:192
  243.5 0.7 slice_reduce_fusion.1
  244.2 1.5 slice_reduce_fusion
  247.0 62.3 %all-to-all-done.2 = bf16[64,4,1024]{2,1,0:T(4,128)(2,1)S(1)} async-done(((bf16[64,4,1024]{2,1,0:T(4,128)(2,1)}), bf16[64,4,1024]{2,1,0:T(4,128)(2,1)S(1)}, u32[]{:S(2)}, u32[]{:S(2)}) %all-to-all-start.2) | async-done | bytes 524320 | tf_op jit(solution)/shard_map/all_to_all | solution.py:192
  309.2 0.1 all_to_all.26
  309.4 0.3 convolution_convert_fusion.7
  309.6 0.0 copy-start.3
  309.6 0.2 conditional.1
  309.9 2.3 collective-permute-start.18
  312.2 8.1 %collective-permute-done.18 = bf16[128,1024]{1,0:T(8,128)(2,1)S(1)} collective-permute-done((bf16[128,1024]{1,0:T(8,128)(2,1)S(1)}, bf16[128,1024]{1,0:T(8,128)(2,1)S(1)}, u32[]{:S(2)}, u32[]{:S(2)}) %collective-permute-start.18) | collective-permute-done | bytes 262176 | tf_op jit(solution)/shard_map/ppermute | solution.py:218
  320.3 2.0 fusion.41
  322.3 0.8 pad_maximum_fusion
  (62 shorter events, 0.8 us)
Async XLA Ops:
  0.6 10.1 %collective-permute-start.1 = (s32[128]{0:T(128)}, s32[128]{0:T(128)S(1)}, u32[]{:S(2)}, u32[]{:S(2)}) collective-permute-start(s32[128]{0:T(128)} %bitcast.13), channel_id=1, source_target_pairs={{0,65},{1,64},{2,67},{3,66},{4,69},{5,68},{6,71},{7,70},{8,73},{9,... | collective-permute-start | bytes 1544 | tf_op jit(solution)/shard_map/ppermute | solution.py:34
  3.5 7.1 %collective-permute-start = (s32[128]{0:T(128)}, s32[128]{0:T(128)S(1)}, u32[]{:S(2)}, u32[]{:S(2)}) collective-permute-start(s32[128]{0:T(128)} %bitcast.14), channel_id=1, source_target_pairs={{0,64},{1,65},{2,66},{3,67},{4,68},{5,69},{6,70},{7,71},{8,72},{9,... | collective-permute-start | bytes 1544 | tf_op jit(solution)/shard_map/ppermute | solution.py:34
  6.9 6.1 %collective-permute-start.2 = (bf16[128,4096]{1,0:T(8,128)(2,1)}, bf16[128,4096]{1,0:T(8,128)(2,1)S(1)}, u32[]{:S(2)}, u32[]{:S(2)}) collective-permute-start(bf16[128,4096]{1,0:T(8,128)(2,1)} %param.7), channel_id=1, source_target_pairs={{0,1},{1,0},{2,3},{3,2},{4,5},{5,4},{6,7},{7,6},{8,9},{9,8},{10,11... | collective-permute-start | bytes 3145736 | tf_op jit(solution)/shard_map/ppermute | solution.py:27
  14.0 72.6 %copy-start.1 = (bf16[216,2048]{1,0:T(8,128)(2,1)}, bf16[216,2048]{1,0:T(8,128)(2,1)S(1)}, u32[]{:S(2)}) copy-start(bf16[216,2048]{1,0:T(8,128)(2,1)S(1)} %convolution_convert_fusion.4) | copy-start | bytes 2654212
  14.1 176.7 %collective-permute-start.9 = (bf16[8,4224]{1,0:T(8,128)(2,1)S(1)}, bf16[8,4224]{1,0:T(8,128)(2,1)S(1)}, u32[]{:S(2)}, u32[]{:S(2)}) collective-permute-start(bf16[8,4224]{1,0:T(8,128)(2,1)S(1)} %pad_maximum_fusion.4), channel_id=1, source_target_pairs={{0,32},{1,33},{2,34},{3,35},{4,36},{5,37},{6,38},{7,39},{8,40},{9,... | collective-permute-start | bytes 202760 | tf_op jit(solution)/shard_map/ppermute | solution.py:27
  43.1 31.0 %collective-permute-start.4 = (bf16[48,2176]{1,0:T(8,128)(2,1)S(1)}, bf16[48,2176]{1,0:T(8,128)(2,1)S(1)}, u32[]{:S(2)}, u32[]{:S(2)}) collective-permute-start(bf16[48,2176]{1,0:T(8,128)(2,1)S(1)} %pad_maximum_fusion.2), channel_id=1, source_target_pairs={{0,16},{1,49},{2,18},{3,51},{4,20},{5,53},{6,22},{7,55},{8,24},{9,... | collective-permute-start | bytes 626696 | tf_op jit(solution)/shard_map/ppermute | solution.py:27
  49.3 31.1 %collective-permute-start.5 = (bf16[48,2176]{1,0:T(8,128)(2,1)S(1)}, bf16[48,2176]{1,0:T(8,128)(2,1)S(1)}, u32[]{:S(2)}, u32[]{:S(2)}) collective-permute-start(bf16[48,2176]{1,0:T(8,128)(2,1)S(1)} %pad_maximum_fusion.3), channel_id=1, source_target_pairs={{0,24},{1,41},{2,26},{3,43},{4,28},{5,45},{6,30},{7,47},{8,32},{9,... | collective-permute-start | bytes 626696 | tf_op jit(solution)/shard_map/ppermute | solution.py:27
  53.1 33.6 %collective-permute-start.3 = (bf16[48,2176]{1,0:T(8,128)(2,1)S(1)}, bf16[48,2176]{1,0:T(8,128)(2,1)S(1)}, u32[]{:S(2)}, u32[]{:S(2)}) collective-permute-start(bf16[48,2176]{1,0:T(8,128)(2,1)S(1)} %pad_maximum_fusion.1), channel_id=1, source_target_pairs={{0,8},{1,57},{2,10},{3,59},{4,12},{5,61},{6,14},{7,63},{8,16},{9,1... | collective-permute-start | bytes 626696 | tf_op jit(solution)/shard_map/ppermute | solution.py:27
  56.6 134.2 %collective-permute-start.13 = (bf16[48,2048]{1,0:T(8,128)(2,1)S(1)}, bf16[48,2048]{1,0:T(8,128)(2,1)S(1)}, u32[]{:S(2)}, u32[]{:S(2)}) collective-permute-start(bf16[48,2048]{1,0:T(8,128)(2,1)S(1)} %get-tuple-element.53), channel_id=1, source_target_pairs={{0,24},{1,41},{2,26},{3,43},{4,28},{5,45},{6,30},{7,47},{8,32},{9,... | collective-permute-start | bytes 589832 | tf_op jit(solution)/shard_map/ppermute | solution.py:27
  74.2 116.7 %collective-permute-start.12 = (bf16[48,2048]{1,0:T(8,128)(2,1)S(1)}, bf16[48,2048]{1,0:T(8,128)(2,1)S(1)}, u32[]{:S(2)}, u32[]{:S(2)}) collective-permute-start(bf16[48,2048]{1,0:T(8,128)(2,1)S(1)} %get-tuple-element.54), channel_id=1, source_target_pairs={{0,16},{1,49},{2,18},{3,51},{4,20},{5,53},{6,22},{7,55},{8,24},{9,... | collective-permute-start | bytes 589832 | tf_op jit(solution)/shard_map/ppermute | solution.py:27
  80.4 110.4 %collective-permute-start.11 = (bf16[48,2048]{1,0:T(8,128)(2,1)S(1)}, bf16[48,2048]{1,0:T(8,128)(2,1)S(1)}, u32[]{:S(2)}, u32[]{:S(2)}) collective-permute-start(bf16[48,2048]{1,0:T(8,128)(2,1)S(1)} %get-tuple-element.55), channel_id=1, source_target_pairs={{0,8},{1,57},{2,10},{3,59},{4,12},{5,61},{6,14},{7,63},{8,16},{9,1... | collective-permute-start | bytes 589832 | tf_op jit(solution)/shard_map/ppermute | solution.py:27
  86.9 120.2 %slice-start.1 = ((s8[8388608]{0:T(1024)(128)(4,1)}), s8[4194304]{0:T(1024)(128)(4,1)S(1)}, s32[]{:S(2)}) async-start(s8[8388608]{0:T(1024)(128)(4,1)} %bitcast.10), calls=%async_computation.4 | async-start | bytes 8388608
  87.4 105.7 %slice-start = ((bf16[216,2048]{1,0:T(8,128)(2,1)}), bf16[64,2048]{1,0:T(8,128)(2,1)S(1)}, s32[]{:S(2)}) async-start(bf16[216,2048]{1,0:T(8,128)(2,1)} %copy-done.1), calls=%async_computation.3 | async-start | bytes 524288 | tf_op jit(solution)/shard_map/slice | solution.py:151
  87.5 73.1 %collective-permute-start.6 = (bf16[64,2176]{1,0:T(8,128)(2,1)S(1)}, bf16[64,2176]{1,0:T(8,128)(2,1)S(1)}, u32[]{:S(2)}, u32[]{:S(2)}) collective-permute-start(bf16[64,2176]{1,0:T(8,128)(2,1)S(1)} %get-tuple-element.44), channel_id=1, source_target_pairs={{0,2},{1,63},{2,4},{3,1},{4,6},{5,3},{6,8},{7,5},{8,10},{9,7},{10,... | collective-permute-start | bytes 835592 | tf_op jit(solution)/shard_map/ppermute | solution.py:27
  160.6 10.7 %collective-permute-start.7 = (bf16[64,2176]{1,0:T(8,128)(2,1)S(1)}, bf16[64,2176]{1,0:T(8,128)(2,1)S(1)}, u32[]{:S(2)}, u32[]{:S(2)}) collective-permute-start(bf16[64,2176]{1,0:T(8,128)(2,1)S(1)} %get-tuple-element.43), channel_id=1, source_target_pairs={{0,4},{1,61},{2,6},{3,63},{4,8},{5,1},{6,10},{7,3},{8,12},{9,5},{1... | collective-permute-start | bytes 835592 | tf_op jit(solution)/shard_map/ppermute | solution.py:27
  171.2 19.5 %collective-permute-start.8 = (bf16[64,2176]{1,0:T(8,128)(2,1)S(1)}, bf16[64,2176]{1,0:T(8,128)(2,1)S(1)}, u32[]{:S(2)}, u32[]{:S(2)}) collective-permute-start(bf16[64,2176]{1,0:T(8,128)(2,1)S(1)} %get-tuple-element.42), channel_id=1, source_target_pairs={{0,6},{1,59},{2,8},{3,61},{4,10},{5,63},{6,12},{7,1},{8,14},{9,3},... | collective-permute-start | bytes 835592 | tf_op jit(solution)/shard_map/ppermute | solution.py:27
  190.8 16.3 %slice-start.2 = ((s8[8388608]{0:T(1024)(128)(4,1)}), s8[4194304]{0:T(1024)(128)(4,1)S(1)}, s32[]{:S(2)}) async-start(s8[8388608]{0:T(1024)(128)(4,1)} %bitcast.10), calls=%async_computation.5 | async-start | bytes 8388608
  190.9 15.3 %collective-permute-start.10 = (bf16[132,2176]{1,0:T(8,128)(2,1)S(1)}, bf16[132,2176]{1,0:T(8,128)(2,1)S(1)}, u32[]{:S(2)}, u32[]{:S(2)}) collective-permute-start(bf16[132,2176]{1,0:T(8,128)(2,1)S(1)} %get-tuple-element.78), channel_id=1, source_target_pairs={{0,1},{1,0},{2,3},{3,2},{4,5},{5,4},{6,7},{7,6},{8,9},{9,8},{10,11... | collective-permute-start | bytes 1723400 | tf_op jit(solution)/shard_map/ppermute | solution.py:27
  193.6 18.5 %collective-permute-start.16 = (bf16[64,2048]{1,0:T(8,128)(2,1)S(1)}, bf16[64,2048]{1,0:T(8,128)(2,1)S(1)}, u32[]{:S(2)}, u32[]{:S(2)}) collective-permute-start(bf16[64,2048]{1,0:T(8,128)(2,1)S(1)} %get-tuple-element.45), channel_id=1, source_target_pairs={{0,6},{1,59},{2,8},{3,61},{4,10},{5,63},{6,12},{7,1},{8,14},{9,3},... | collective-permute-start | bytes 786440 | tf_op jit(solution)/shard_map/ppermute | solution.py:27
  196.2 18.5 %collective-permute-start.15 = (bf16[64,2048]{1,0:T(8,128)(2,1)S(1)}, bf16[64,2048]{1,0:T(8,128)(2,1)S(1)}, u32[]{:S(2)}, u32[]{:S(2)}) collective-permute-start(bf16[64,2048]{1,0:T(8,128)(2,1)S(1)} %get-tuple-element.46), channel_id=1, source_target_pairs={{0,4},{1,61},{2,6},{3,63},{4,8},{5,1},{6,10},{7,3},{8,12},{9,5},{1... | collective-permute-start | bytes 786440 | tf_op jit(solution)/shard_map/ppermute | solution.py:27
  199.6 18.7 %collective-permute-start.14 = (bf16[64,2048]{1,0:T(8,128)(2,1)S(1)}, bf16[64,2048]{1,0:T(8,128)(2,1)S(1)}, u32[]{:S(2)}, u32[]{:S(2)}) collective-permute-start(bf16[64,2048]{1,0:T(8,128)(2,1)S(1)} %get-tuple-element.47), channel_id=1, source_target_pairs={{0,2},{1,63},{2,4},{3,1},{4,6},{5,3},{6,8},{7,5},{8,10},{9,7},{10,... | collective-permute-start | bytes 786440 | tf_op jit(solution)/shard_map/ppermute | solution.py:27
  206.2 0.8 copy-start.2
  218.5 3.9 %collective-permute-start.17 = (bf16[132,2048]{1,0:T(8,128)(2,1)S(1)}, bf16[132,2048]{1,0:T(8,128)(2,1)S(1)}, u32[]{:S(2)}, u32[]{:S(2)}) collective-permute-start(bf16[132,2048]{1,0:T(8,128)(2,1)S(1)} %get-tuple-element.76), channel_id=1, source_target_pairs={{0,1},{1,0},{2,3},{3,2},{4,5},{5,4},{6,7},{7,6},{8,9},{9,8},{10,11... | collective-permute-start | bytes 1622024 | tf_op jit(solution)/shard_map/ppermute | solution.py:27
  228.1 81.3 %copy-start = (bf16[128,4096]{1,0:T(8,128)(2,1)S(1)}, bf16[128,4096]{1,0:T(8,128)(2,1)}, u32[]{:S(2)}) copy-start(bf16[128,4096]{1,0:T(8,128)(2,1)} %param.7) | copy-start | bytes 3145732
  230.2 79.0 %all-to-all-start.2 = ((bf16[64,4,1024]{2,1,0:T(4,128)(2,1)}), bf16[64,4,1024]{2,1,0:T(4,128)(2,1)S(1)}, u32[]{:S(2)}, u32[]{:S(2)}) async-start(bf16[64,4,1024]{2,1,0:T(4,128)(2,1)} %all_to_all.24), calls=%async_computation.2 | async-start | bytes 1048576 | tf_op jit(solution)/shard_map/all_to_all | solution.py:192
  309.6 10.7 %copy-start.3 = (f32[128]{0:T(128)S(1)}, f32[128]{0:T(128)}, u32[]{:S(2)}) copy-start(f32[128]{0:T(128)} %param.9) | copy-start | bytes 1540
  309.9 10.5 %collective-permute-start.18 = (bf16[128,1024]{1,0:T(8,128)(2,1)S(1)}, bf16[128,1024]{1,0:T(8,128)(2,1)S(1)}, u32[]{:S(2)}, u32[]{:S(2)}) collective-permute-start(bf16[128,1024]{1,0:T(8,128)(2,1)S(1)} %get-tuple-element.91), channel_id=1, source_target_pairs={{64,0},{128,64},{192,128},{256,192},{320,256},{384,320},{448,384},... | collective-permute-start | bytes 786440 | tf_op jit(solution)/shard_map/ppermute | solution.py:218

commit v2 on v1

--- a/solution.py
+++ b/solution.py
@@ -178,25 +178,25 @@
         )
     products = products.astype(jnp.bfloat16)
 
-    spot = numbers(kept.shape[0])
-    main = spot < NEAR * step // 2
-    far = jnp.where(main, (spot % (step // 2)) // PAIR * NEAR + spot // (step // 2), half)
-    other = jnp.where(main, (spot // SLOTS) % 2, 0)
-
-    def target(lane):
-        sign = 1 - 2 * lane
-        return (((chip - sign * far) % chips) * 2 + (lane + other) % 2) * SLOTS + spot % SLOTS
-
-    targets = jnp.concatenate([target(core), target(1 - core)])
-    places = numbers(experts * SLOTS)
-    returned = lax.all_to_all(
-        picked(onehot(places, targets), products),
-        "expert",
-        split_axis=0,
-        concat_axis=0,
-        tiled=True,
-    )
-    return picked(onehot(expert * SLOTS + rank, places), returned), seen
+    part = products.shape[0] // 2
+    stay = products[:part]
+    gone = moved(products[part:], flip=True)
+    pieces = []
+    for b in range(NEAR):
+        cell = slice(b * side, (b + 1) * side)
+        piece = jnp.concatenate([stay[cell], gone[cell]], axis=0)
+        pieces.append(moved(piece, chip_step=-b) if b else piece)
+    piece = jnp.concatenate([stay[NEAR * side :], gone[NEAR * side :]], axis=0)
+    over_back = moved(piece, chip_step=-half)
+    relayed = picked(relay_pick.T, jnp.concatenate(pieces, axis=0))
+    final = [relayed[:BLOCK]]
+    for a in range(1, blocks):
+        piece = relayed[BLOCK + (a - 1) * PACKED : BLOCK + a * PACKED]
+        final.append(moved(piece, chip_step=-a * NEAR))
+    final = jnp.concatenate(final + [over_back], axis=0)
+    own = picked(send_pick[:, :tokens].T, final)
+    other = picked(send_pick[:, tokens:].T, final)
+    return own + moved(other, flip=True), seen
 
 
 def local(cotangent, expert_ids, route_weight, saved_preact, down_weight):

time: 324 us -> 330 us (1.019)
  the two profiles are of different devices: /device:TPU:14 before, /device:TPU:62 now
where the time goes in v2:
time: 330 us; the launch traced here: 329 us
  starting transfers between devices  159 us (48%)
  waiting for transfers between devices  142 us (43%)
  local copies, waits for them, and re-layouts  8.62 us (3%)
  other arithmetic  8.29 us (3%)
  matrix products  7.45 us (2%)
  between operations  3.46 us (1%)
    ppermute x25, starting transfers between devices, moved(): lax.ppermute(block, 'expert', [(i, target(i)) for i in range(experts)])  152 us
    ppermute x25, waiting for transfers between devices, moved(): lax.ppermute(block, 'expert', [(i, target(i)) for i in range(experts)])  130 us
    ppermute x1, waiting for transfers between devices, local(): back_hidden = lax.ppermute(result, 'section', route)  12.2 us
  transfers between devices with their start and end apart: 28, of which 13 were waited for; matrix products, arithmetic and copies ran while one was open for 3% of the time, Pallas kernels for 0%

profile of v2, /device:TPU:62, one launch (start us, length us, event | category | flops | bytes accessed | tf_op | source)
XLA Modules:
  0.0 329.4 jit_solution(430073407895830576)
XLA Ops:
  0.6 1.9 collective-permute-start.1
  2.6 3.0 collective-permute-start
  5.5 2.3 collective-permute-start.2
  7.9 1.3 fusion.86
  9.4 0.6 reduce_max.27
  11.1 0.2 convert_reduce_fusion
  11.8 0.4 convolution_convert_fusion.5
  12.3 0.4 convolution_convert_fusion.4
  12.8 28.1 %collective-permute-start.9 = (bf16[8,4224]{1,0:T(8,128)(2,1)S(1)}, bf16[8,4224]{1,0:T(8,128)(2,1)S(1)}, u32[]{:S(2)}, u32[]{:S(2)}) collective-permute-start(bf16[8,4224]{1,0:T(8,128)(2,1)S(1)} %pad_maximum_fusion.7), channel_id=1, source_target_pairs={{0,32},{1,33},{2,34},{3,35},{4,36},{5,37},{6,38},{7,39},{8,40},{9,... | collective-permute-start | bytes 202760 | tf_op jit(solution)/shard_map/ppermute | solution.py:27
  40.9 6.1 %collective-permute-start.4 = (bf16[48,2176]{1,0:T(8,128)(2,1)S(1)}, bf16[48,2176]{1,0:T(8,128)(2,1)S(1)}, u32[]{:S(2)}, u32[]{:S(2)}) collective-permute-start(bf16[48,2176]{1,0:T(8,128)(2,1)S(1)} %pad_maximum_fusion.2), channel_id=1, source_target_pairs={{0,16},{1,49},{2,18},{3,51},{4,20},{5,53},{6,22},{7,55},{8,24},{9,... | collective-permute-start | bytes 626696 | tf_op jit(solution)/shard_map/ppermute | solution.py:27
  47.0 3.7 %collective-permute-start.5 = (bf16[48,2176]{1,0:T(8,128)(2,1)S(1)}, bf16[48,2176]{1,0:T(8,128)(2,1)S(1)}, u32[]{:S(2)}, u32[]{:S(2)}) collective-permute-start(bf16[48,2176]{1,0:T(8,128)(2,1)S(1)} %pad_maximum_fusion.3), channel_id=1, source_target_pairs={{0,24},{1,41},{2,26},{3,43},{4,28},{5,45},{6,30},{7,47},{8,32},{9,... | collective-permute-start | bytes 626696 | tf_op jit(solution)/shard_map/ppermute | solution.py:27
  50.8 4.4 %collective-permute-start.3 = (bf16[48,2176]{1,0:T(8,128)(2,1)S(1)}, bf16[48,2176]{1,0:T(8,128)(2,1)S(1)}, u32[]{:S(2)}, u32[]{:S(2)}) collective-permute-start(bf16[48,2176]{1,0:T(8,128)(2,1)S(1)} %pad_maximum_fusion.1), channel_id=1, source_target_pairs={{0,8},{1,57},{2,10},{3,59},{4,12},{5,61},{6,14},{7,63},{8,16},{9,1... | collective-permute-start | bytes 626696 | tf_op jit(solution)/shard_map/ppermute | solution.py:27
  55.3 16.6 %collective-permute-start.13 = (bf16[48,2048]{1,0:T(8,128)(2,1)S(1)}, bf16[48,2048]{1,0:T(8,128)(2,1)S(1)}, u32[]{:S(2)}, u32[]{:S(2)}) collective-permute-start(bf16[48,2048]{1,0:T(8,128)(2,1)S(1)} %get-tuple-element.60), channel_id=1, source_target_pairs={{0,24},{1,41},{2,26},{3,43},{4,28},{5,45},{6,30},{7,47},{8,32},{9,... | collective-permute-start | bytes 589832 | tf_op jit(solution)/shard_map/ppermute | solution.py:27
  71.9 39.6 %collective-permute-done.4 = bf16[48,2176]{1,0:T(8,128)(2,1)S(1)} collective-permute-done((bf16[48,2176]{1,0:T(8,128)(2,1)S(1)}, bf16[48,2176]{1,0:T(8,128)(2,1)S(1)}, u32[]{:S(2)}, u32[]{:S(2)}) %collective-permute-start.4) | collective-permute-done | bytes 208928 | tf_op jit(solution)/shard_map/ppermute | solution.py:27
  111.5 5.6 %collective-permute-start.12 = (bf16[48,2048]{1,0:T(8,128)(2,1)S(1)}, bf16[48,2048]{1,0:T(8,128)(2,1)S(1)}, u32[]{:S(2)}, u32[]{:S(2)}) collective-permute-start(bf16[48,2048]{1,0:T(8,128)(2,1)S(1)} %get-tuple-element.61), channel_id=1, source_target_pairs={{0,16},{1,49},{2,18},{3,51},{4,20},{5,53},{6,22},{7,55},{8,24},{9,... | collective-permute-start | bytes 589832 | tf_op jit(solution)/shard_map/ppermute | solution.py:27
  117.3 7.2 %collective-permute-done.5 = bf16[48,2176]{1,0:T(8,128)(2,1)S(1)} collective-permute-done((bf16[48,2176]{1,0:T(8,128)(2,1)S(1)}, bf16[48,2176]{1,0:T(8,128)(2,1)S(1)}, u32[]{:S(2)}, u32[]{:S(2)}) %collective-permute-start.5) | collective-permute-done | bytes 208928 | tf_op jit(solution)/shard_map/ppermute | solution.py:27
  124.5 10.0 %collective-permute-start.11 = (bf16[48,2048]{1,0:T(8,128)(2,1)S(1)}, bf16[48,2048]{1,0:T(8,128)(2,1)S(1)}, u32[]{:S(2)}, u32[]{:S(2)}) collective-permute-start(bf16[48,2048]{1,0:T(8,128)(2,1)S(1)} %get-tuple-element.62), channel_id=1, source_target_pairs={{0,8},{1,57},{2,10},{3,59},{4,12},{5,61},{6,14},{7,63},{8,16},{9,1... | collective-permute-start | bytes 589832 | tf_op jit(solution)/shard_map/ppermute | solution.py:27
  134.9 0.5 fusion.6
  135.5 2.1 collective-permute-start.6
  137.6 21.2 %collective-permute-done.6 = bf16[64,2176]{1,0:T(8,128)(2,1)S(1)} collective-permute-done((bf16[64,2176]{1,0:T(8,128)(2,1)S(1)}, bf16[64,2176]{1,0:T(8,128)(2,1)S(1)}, u32[]{:S(2)}, u32[]{:S(2)}) %collective-permute-start.6) | collective-permute-done | bytes 278560 | tf_op jit(solution)/shard_map/ppermute | solution.py:27
  158.8 3.0 collective-permute-start.7
  161.9 10.4 %collective-permute-done.7 = bf16[64,2176]{1,0:T(8,128)(2,1)S(1)} collective-permute-done((bf16[64,2176]{1,0:T(8,128)(2,1)S(1)}, bf16[64,2176]{1,0:T(8,128)(2,1)S(1)}, u32[]{:S(2)}, u32[]{:S(2)}) %collective-permute-start.7) | collective-permute-done | bytes 278560 | tf_op jit(solution)/shard_map/ppermute | solution.py:27
  172.3 5.1 %collective-permute-start.8 = (bf16[64,2176]{1,0:T(8,128)(2,1)S(1)}, bf16[64,2176]{1,0:T(8,128)(2,1)S(1)}, u32[]{:S(2)}, u32[]{:S(2)}) collective-permute-start(bf16[64,2176]{1,0:T(8,128)(2,1)S(1)} %get-tuple-element.49), channel_id=1, source_target_pairs={{0,6},{1,59},{2,8},{3,61},{4,10},{5,63},{6,12},{7,1},{8,14},{9,3},... | collective-permute-start | bytes 835592 | tf_op jit(solution)/shard_map/ppermute | solution.py:27
  177.5 12.0 %collective-permute-done.8 = bf16[64,2176]{1,0:T(8,128)(2,1)S(1)} collective-permute-done((bf16[64,2176]{1,0:T(8,128)(2,1)S(1)}, bf16[64,2176]{1,0:T(8,128)(2,1)S(1)}, u32[]{:S(2)}, u32[]{:S(2)}) %collective-permute-start.8) | collective-permute-done | bytes 278560 | tf_op jit(solution)/shard_map/ppermute | solution.py:27
  189.6 2.2 collective-permute-start.10
  191.8 0.4 convolution_convert_fusion.3
  192.3 3.2 collective-permute-start.16
  195.5 5.8 %collective-permute-start.15 = (bf16[64,2048]{1,0:T(8,128)(2,1)S(1)}, bf16[64,2048]{1,0:T(8,128)(2,1)S(1)}, u32[]{:S(2)}, u32[]{:S(2)}) collective-permute-start(bf16[64,2048]{1,0:T(8,128)(2,1)S(1)} %get-tuple-element.53), channel_id=1, source_target_pairs={{0,4},{1,61},{2,6},{3,63},{4,8},{5,1},{6,10},{7,3},{8,12},{9,5},{1... | collective-permute-start | bytes 786440 | tf_op jit(solution)/shard_map/ppermute | solution.py:27
  201.3 1.9 collective-permute-start.14
  203.4 0.8 copy-done.2
  204.2 1.3 fusion.4
  205.5 2.5 collective-permute-done.16
  208.0 5.9 %collective-permute-done.15 = bf16[64,2048]{1,0:T(8,128)(2,1)S(1)} collective-permute-done((bf16[64,2048]{1,0:T(8,128)(2,1)S(1)}, bf16[64,2048]{1,0:T(8,128)(2,1)S(1)}, u32[]{:S(2)}, u32[]{:S(2)}) %collective-permute-start.15) | collective-permute-done | bytes 262176 | tf_op jit(solution)/shard_map/ppermute | solution.py:27
  214.0 0.7 slice_dynamic-update-slice_fusion.11
  214.7 0.7 slice_dynamic-update-slice_fusion.10
  215.3 0.7 slice_dynamic-update-slice_fusion.9
  216.0 2.1 collective-permute-start.17
  218.2 1.7 collective-permute-done.17
  219.9 3.6 %concatenate.196 = bf16[264,2048]{1,0:T(8,128)(2,1)S(1)} concatenate(bf16[32,2048]{1,0:T(8,128)(2,1)S(1)} %get-tuple-element.93, bf16[32,2048]{1,0:T(8,128)(2,1)} %get-tuple-element.91, bf16[32,2048]{1,0:T(8,128)(2,1)} %get-tuple-element.89, bf16[32,2048]{1,0:T(8,128)(2,1)} %get-tuple-element.87, bf16[4,2048]{1,0:T(4,128)(2,1)S(1)} %get-tuple-element.95, ...), dimensions={0} | concatenate | bytes 2162688 | tf_op jit(solution)/shard_map/concatenate | solution.py:174
  223.5 3.5 %fusion.2 = f32[264,1024]{1,0:T(8,128)S(1)} fusion(bf16[264,2048]{1,0:T(8,128)(2,1)S(1)} %concatenate.196, bf16[1024,4096]{1,0:T(8,128)(2,1)} %bitcast.10), kind=kOutput, calls=%fused_computation.9 | convolution fusion | flops 1107296256 | bytes 6356992 | tf_op jit(solution)/shard_map/dot_general | solution.py:176
  227.3 2.1 collective-permute-start.18
  229.4 0.7 slice_reduce_fusion.1
  230.1 0.6 collective-permute-done.18
  230.7 13.3 %collective-permute-start.25 = (bf16[8,1024]{1,0:T(8,128)(2,1)S(1)}, bf16[8,1024]{1,0:T(8,128)(2,1)S(1)}, u32[]{:S(2)}, u32[]{:S(2)}) collective-permute-start(bf16[8,1024]{1,0:T(8,128)(2,1)S(1)} %pad_maximum_fusion.8), channel_id=1, source_target_pairs={{0,32},{1,33},{2,34},{3,35},{4,36},{5,37},{6,38},{7,39},{8,40},{9,... | collective-permute-start | bytes 49160 | tf_op jit(solution)/shard_map/ppermute | solution.py:27
  244.1 4.2 %collective-permute-start.19 = (bf16[64,1024]{1,0:T(8,128)(2,1)S(1)}, bf16[64,1024]{1,0:T(8,128)(2,1)S(1)}, u32[]{:S(2)}, u32[]{:S(2)}) collective-permute-start(bf16[64,1024]{1,0:T(8,128)(2,1)S(1)} %pad_maximum_fusion.4), channel_id=1, source_target_pairs={{0,62},{1,3},{2,0},{3,5},{4,2},{5,7},{6,4},{7,9},{8,6},{9,11},{10,... | collective-permute-start | bytes 393224 | tf_op jit(solution)/shard_map/ppermute | solution.py:27
  248.3 4.1 %collective-permute-start.20 = (bf16[64,1024]{1,0:T(8,128)(2,1)S(1)}, bf16[64,1024]{1,0:T(8,128)(2,1)S(1)}, u32[]{:S(2)}, u32[]{:S(2)}) collective-permute-start(bf16[64,1024]{1,0:T(8,128)(2,1)S(1)} %pad_maximum_fusion.5), channel_id=1, source_target_pairs={{0,60},{1,5},{2,62},{3,7},{4,0},{5,9},{6,2},{7,11},{8,4},{9,13},{1... | collective-permute-start | bytes 393224 | tf_op jit(solution)/shard_map/ppermute | solution.py:27
  252.4 4.1 %collective-permute-start.21 = (bf16[64,1024]{1,0:T(8,128)(2,1)S(1)}, bf16[64,1024]{1,0:T(8,128)(2,1)S(1)}, u32[]{:S(2)}, u32[]{:S(2)}) collective-permute-start(bf16[64,1024]{1,0:T(8,128)(2,1)S(1)} %pad_maximum_fusion.6), channel_id=1, source_target_pairs={{0,58},{1,7},{2,60},{3,9},{4,62},{5,11},{6,0},{7,13},{8,2},{9,15},... | collective-permute-start | bytes 393224 | tf_op jit(solution)/shard_map/ppermute | solution.py:27
  256.5 0.3 collective-permute-done.20
  256.9 5.5 %collective-permute-done.21 = bf16[64,1024]{1,0:T(8,128)(2,1)S(1)} collective-permute-done((bf16[64,1024]{1,0:T(8,128)(2,1)S(1)}, bf16[64,1024]{1,0:T(8,128)(2,1)S(1)}, u32[]{:S(2)}, u32[]{:S(2)}) %collective-permute-start.21) | collective-permute-done | bytes 131104 | tf_op jit(solution)/shard_map/ppermute | solution.py:27
  262.4 0.3 convolution_convert_fusion.6
  262.8 4.9 %collective-permute-start.22 = (bf16[48,1024]{1,0:T(8,128)(2,1)S(1)}, bf16[48,1024]{1,0:T(8,128)(2,1)S(1)}, u32[]{:S(2)}, u32[]{:S(2)}) collective-permute-start(bf16[48,1024]{1,0:T(8,128)(2,1)S(1)} %get-tuple-element.75), channel_id=1, source_target_pairs={{0,56},{1,9},{2,58},{3,11},{4,60},{5,13},{6,62},{7,15},{8,0},{9,17... | collective-permute-start | bytes 294920 | tf_op jit(solution)/shard_map/ppermute | solution.py:27
  267.7 8.1 %collective-permute-start.24 = (bf16[48,1024]{1,0:T(8,128)(2,1)S(1)}, bf16[48,1024]{1,0:T(8,128)(2,1)S(1)}, u32[]{:S(2)}, u32[]{:S(2)}) collective-permute-start(bf16[48,1024]{1,0:T(8,128)(2,1)S(1)} %get-tuple-element.73), channel_id=1, source_target_pairs={{0,40},{1,25},{2,42},{3,27},{4,44},{5,29},{6,46},{7,31},{8,48},{9,... | collective-permute-start | bytes 294920 | tf_op jit(solution)/shard_map/ppermute | solution.py:27
  275.9 7.4 %collective-permute-start.23 = (bf16[48,1024]{1,0:T(8,128)(2,1)S(1)}, bf16[48,1024]{1,0:T(8,128)(2,1)S(1)}, u32[]{:S(2)}, u32[]{:S(2)}) collective-permute-start(bf16[48,1024]{1,0:T(8,128)(2,1)S(1)} %get-tuple-element.74), channel_id=1, source_target_pairs={{0,48},{1,17},{2,50},{3,19},{4,52},{5,21},{6,54},{7,23},{8,56},{9,... | collective-permute-start | bytes 294920 | tf_op jit(solution)/shard_map/ppermute | solution.py:27
  283.3 23.0 %collective-permute-done.23 = bf16[48,1024]{1,0:T(8,128)(2,1)S(1)} collective-permute-done((bf16[48,1024]{1,0:T(8,128)(2,1)S(1)}, bf16[48,1024]{1,0:T(8,128)(2,1)S(1)}, u32[]{:S(2)}, u32[]{:S(2)}) %collective-permute-start.23) | collective-permute-done | bytes 98336 | tf_op jit(solution)/shard_map/ppermute | solution.py:27
  306.3 0.3 convolution_convert_fusion.7
  306.6 1.9 collective-permute-start.26
  308.5 1.5 slice_reduce_fusion
  311.3 0.3 convolution_convert_fusion.8
  311.6 0.8 conditional.1
  311.6 0.8 add.371
  312.4 1.9 collective-permute-start.27
  314.3 12.2 %collective-permute-done.27 = bf16[128,1024]{1,0:T(8,128)(2,1)S(1)} collective-permute-done((bf16[128,1024]{1,0:T(8,128)(2,1)}, bf16[128,1024]{1,0:T(8,128)(2,1)S(1)}, u32[]{:S(2)}, u32[]{:S(2)}) %collective-permute-start.27) | collective-permute-done | bytes 262176 | tf_op jit(solution)/shard_map/ppermute | solution.py:218
  326.5 2.0 fusion.37
  328.5 0.8 pad_maximum_fusion
  (97 shorter events, 2.8 us)
Async XLA Ops:
  0.6 8.6 %collective-permute-start.1 = (s32[128]{0:T(128)}, s32[128]{0:T(128)S(1)}, u32[]{:S(2)}, u32[]{:S(2)}) collective-permute-start(s32[128]{0:T(128)} %bitcast.15), channel_id=1, source_target_pairs={{0,65},{1,64},{2,67},{3,66},{4,69},{5,68},{6,71},{7,70},{8,73},{9,... | collective-permute-start | bytes 1544 | tf_op jit(solution)/shard_map/ppermute | solution.py:34
  2.6 6.6 %collective-permute-start = (s32[128]{0:T(128)}, s32[128]{0:T(128)S(1)}, u32[]{:S(2)}, u32[]{:S(2)}) collective-permute-start(s32[128]{0:T(128)} %bitcast.16), channel_id=1, source_target_pairs={{0,64},{1,65},{2,66},{3,67},{4,68},{5,69},{6,70},{7,71},{8,72},{9,... | collective-permute-start | bytes 1544 | tf_op jit(solution)/shard_map/ppermute | solution.py:34
  5.5 6.1 %collective-permute-start.2 = (bf16[128,4096]{1,0:T(8,128)(2,1)}, bf16[128,4096]{1,0:T(8,128)(2,1)S(1)}, u32[]{:S(2)}, u32[]{:S(2)}) collective-permute-start(bf16[128,4096]{1,0:T(8,128)(2,1)} %param.7), channel_id=1, source_target_pairs={{0,1},{1,0},{2,3},{3,2},{4,5},{5,4},{6,7},{7,6},{8,9},{9,8},{10,11... | collective-permute-start | bytes 3145736 | tf_op jit(solution)/shard_map/ppermute | solution.py:27
  12.7 122.0 %copy-start.1 = (bf16[216,2048]{1,0:T(8,128)(2,1)}, bf16[216,2048]{1,0:T(8,128)(2,1)S(1)}, u32[]{:S(2)}) copy-start(bf16[216,2048]{1,0:T(8,128)(2,1)S(1)} %convolution_convert_fusion.4) | copy-start | bytes 2654212
  12.8 176.8 %collective-permute-start.9 = (bf16[8,4224]{1,0:T(8,128)(2,1)S(1)}, bf16[8,4224]{1,0:T(8,128)(2,1)S(1)}, u32[]{:S(2)}, u32[]{:S(2)}) collective-permute-start(bf16[8,4224]{1,0:T(8,128)(2,1)S(1)} %pad_maximum_fusion.7), channel_id=1, source_target_pairs={{0,32},{1,33},{2,34},{3,35},{4,36},{5,37},{6,38},{7,39},{8,40},{9,... | collective-permute-start | bytes 202760 | tf_op jit(solution)/shard_map/ppermute | solution.py:27
  40.9 70.6 %collective-permute-start.4 = (bf16[48,2176]{1,0:T(8,128)(2,1)S(1)}, bf16[48,2176]{1,0:T(8,128)(2,1)S(1)}, u32[]{:S(2)}, u32[]{:S(2)}) collective-permute-start(bf16[48,2176]{1,0:T(8,128)(2,1)S(1)} %pad_maximum_fusion.2), channel_id=1, source_target_pairs={{0,16},{1,49},{2,18},{3,51},{4,20},{5,53},{6,22},{7,55},{8,24},{9,... | collective-permute-start | bytes 626696 | tf_op jit(solution)/shard_map/ppermute | solution.py:27
  47.0 77.4 %collective-permute-start.5 = (bf16[48,2176]{1,0:T(8,128)(2,1)S(1)}, bf16[48,2176]{1,0:T(8,128)(2,1)S(1)}, u32[]{:S(2)}, u32[]{:S(2)}) collective-permute-start(bf16[48,2176]{1,0:T(8,128)(2,1)S(1)} %pad_maximum_fusion.3), channel_id=1, source_target_pairs={{0,24},{1,41},{2,26},{3,43},{4,28},{5,45},{6,30},{7,47},{8,32},{9,... | collective-permute-start | bytes 626696 | tf_op jit(solution)/shard_map/ppermute | solution.py:27
  50.8 83.8 %collective-permute-start.3 = (bf16[48,2176]{1,0:T(8,128)(2,1)S(1)}, bf16[48,2176]{1,0:T(8,128)(2,1)S(1)}, u32[]{:S(2)}, u32[]{:S(2)}) collective-permute-start(bf16[48,2176]{1,0:T(8,128)(2,1)S(1)} %pad_maximum_fusion.1), channel_id=1, source_target_pairs={{0,8},{1,57},{2,10},{3,59},{4,12},{5,61},{6,14},{7,63},{8,16},{9,1... | collective-permute-start | bytes 626696 | tf_op jit(solution)/shard_map/ppermute | solution.py:27
  55.3 134.3 %collective-permute-start.13 = (bf16[48,2048]{1,0:T(8,128)(2,1)S(1)}, bf16[48,2048]{1,0:T(8,128)(2,1)S(1)}, u32[]{:S(2)}, u32[]{:S(2)}) collective-permute-start(bf16[48,2048]{1,0:T(8,128)(2,1)S(1)} %get-tuple-element.60), channel_id=1, source_target_pairs={{0,24},{1,41},{2,26},{3,43},{4,28},{5,45},{6,30},{7,47},{8,32},{9,... | collective-permute-start | bytes 589832 | tf_op jit(solution)/shard_map/ppermute | solution.py:27
  111.5 78.0 %collective-permute-start.12 = (bf16[48,2048]{1,0:T(8,128)(2,1)S(1)}, bf16[48,2048]{1,0:T(8,128)(2,1)S(1)}, u32[]{:S(2)}, u32[]{:S(2)}) collective-permute-start(bf16[48,2048]{1,0:T(8,128)(2,1)S(1)} %get-tuple-element.61), channel_id=1, source_target_pairs={{0,16},{1,49},{2,18},{3,51},{4,20},{5,53},{6,22},{7,55},{8,24},{9,... | collective-permute-start | bytes 589832 | tf_op jit(solution)/shard_map/ppermute | solution.py:27
  124.5 65.1 %collective-permute-start.11 = (bf16[48,2048]{1,0:T(8,128)(2,1)S(1)}, bf16[48,2048]{1,0:T(8,128)(2,1)S(1)}, u32[]{:S(2)}, u32[]{:S(2)}) collective-permute-start(bf16[48,2048]{1,0:T(8,128)(2,1)S(1)} %get-tuple-element.62), channel_id=1, source_target_pairs={{0,8},{1,57},{2,10},{3,59},{4,12},{5,61},{6,14},{7,63},{8,16},{9,1... | collective-permute-start | bytes 589832 | tf_op jit(solution)/shard_map/ppermute | solution.py:27
  134.9 69.2 %slice-start.1 = ((s8[8388608]{0:T(1024)(128)(4,1)}), s8[4194304]{0:T(1024)(128)(4,1)S(1)}, s32[]{:S(2)}) async-start(s8[8388608]{0:T(1024)(128)(4,1)} %bitcast.12), calls=%async_computation.3 | async-start | bytes 8388608
  135.4 56.4 %slice-start = ((bf16[216,2048]{1,0:T(8,128)(2,1)}), bf16[64,2048]{1,0:T(8,128)(2,1)S(1)}, s32[]{:S(2)}) async-start(bf16[216,2048]{1,0:T(8,128)(2,1)} %copy-done.1), calls=%async_computation.2 | async-start | bytes 524288 | tf_op jit(solution)/shard_map/slice | solution.py:151
  135.5 23.3 %collective-permute-start.6 = (bf16[64,2176]{1,0:T(8,128)(2,1)S(1)}, bf16[64,2176]{1,0:T(8,128)(2,1)S(1)}, u32[]{:S(2)}, u32[]{:S(2)}) collective-permute-start(bf16[64,2176]{1,0:T(8,128)(2,1)S(1)} %get-tuple-element.51), channel_id=1, source_target_pairs={{0,2},{1,63},{2,4},{3,1},{4,6},{5,3},{6,8},{7,5},{8,10},{9,7},{10,... | collective-permute-start | bytes 835592 | tf_op jit(solution)/shard_map/ppermute | solution.py:27
  158.8 13.5 %collective-permute-start.7 = (bf16[64,2176]{1,0:T(8,128)(2,1)S(1)}, bf16[64,2176]{1,0:T(8,128)(2,1)S(1)}, u32[]{:S(2)}, u32[]{:S(2)}) collective-permute-start(bf16[64,2176]{1,0:T(8,128)(2,1)S(1)} %get-tuple-element.50), channel_id=1, source_target_pairs={{0,4},{1,61},{2,6},{3,63},{4,8},{5,1},{6,10},{7,3},{8,12},{9,5},{1... | collective-permute-start | bytes 835592 | tf_op jit(solution)/shard_map/ppermute | solution.py:27
  172.3 17.1 %collective-permute-start.8 = (bf16[64,2176]{1,0:T(8,128)(2,1)S(1)}, bf16[64,2176]{1,0:T(8,128)(2,1)S(1)}, u32[]{:S(2)}, u32[]{:S(2)}) collective-permute-start(bf16[64,2176]{1,0:T(8,128)(2,1)S(1)} %get-tuple-element.49), channel_id=1, source_target_pairs={{0,6},{1,59},{2,8},{3,61},{4,10},{5,63},{6,12},{7,1},{8,14},{9,3},... | collective-permute-start | bytes 835592 | tf_op jit(solution)/shard_map/ppermute | solution.py:27
  189.5 14.7 %slice-start.2 = ((s8[8388608]{0:T(1024)(128)(4,1)}), s8[4194304]{0:T(1024)(128)(4,1)S(1)}, s32[]{:S(2)}) async-start(s8[8388608]{0:T(1024)(128)(4,1)} %bitcast.12), calls=%async_computation.4 | async-start | bytes 8388608
  189.6 13.7 %collective-permute-start.10 = (bf16[132,2176]{1,0:T(8,128)(2,1)S(1)}, bf16[132,2176]{1,0:T(8,128)(2,1)S(1)}, u32[]{:S(2)}, u32[]{:S(2)}) collective-permute-start(bf16[132,2176]{1,0:T(8,128)(2,1)S(1)} %get-tuple-element.96), channel_id=1, source_target_pairs={{0,1},{1,0},{2,3},{3,2},{4,5},{5,4},{6,7},{7,6},{8,9},{9,8},{10,11... | collective-permute-start | bytes 1723400 | tf_op jit(solution)/shard_map/ppermute | solution.py:27
  192.3 15.7 %collective-permute-start.16 = (bf16[64,2048]{1,0:T(8,128)(2,1)S(1)}, bf16[64,2048]{1,0:T(8,128)(2,1)S(1)}, u32[]{:S(2)}, u32[]{:S(2)}) collective-permute-start(bf16[64,2048]{1,0:T(8,128)(2,1)S(1)} %get-tuple-element.52), channel_id=1, source_target_pairs={{0,6},{1,59},{2,8},{3,61},{4,10},{5,63},{6,12},{7,1},{8,14},{9,3},... | collective-permute-start | bytes 786440 | tf_op jit(solution)/shard_map/ppermute | solution.py:27
  195.5 18.4 %collective-permute-start.15 = (bf16[64,2048]{1,0:T(8,128)(2,1)S(1)}, bf16[64,2048]{1,0:T(8,128)(2,1)S(1)}, u32[]{:S(2)}, u32[]{:S(2)}) collective-permute-start(bf16[64,2048]{1,0:T(8,128)(2,1)S(1)} %get-tuple-element.53), channel_id=1, source_target_pairs={{0,4},{1,61},{2,6},{3,63},{4,8},{5,1},{6,10},{7,3},{8,12},{9,5},{1... | collective-permute-start | bytes 786440 | tf_op jit(solution)/shard_map/ppermute | solution.py:27
  201.3 12.7 %collective-permute-start.14 = (bf16[64,2048]{1,0:T(8,128)(2,1)S(1)}, bf16[64,2048]{1,0:T(8,128)(2,1)S(1)}, u32[]{:S(2)}, u32[]{:S(2)}) collective-permute-start(bf16[64,2048]{1,0:T(8,128)(2,1)S(1)} %get-tuple-element.54), channel_id=1, source_target_pairs={{0,2},{1,63},{2,4},{3,1},{4,6},{5,3},{6,8},{7,5},{8,10},{9,7},{10,... | collective-permute-start | bytes 786440 | tf_op jit(solution)/shard_map/ppermute | solution.py:27
  203.3 0.9 copy-start.2
  216.0 3.8 %collective-permute-start.17 = (bf16[132,2048]{1,0:T(8,128)(2,1)S(1)}, bf16[132,2048]{1,0:T(8,128)(2,1)S(1)}, u32[]{:S(2)}, u32[]{:S(2)}) collective-permute-start(bf16[132,2048]{1,0:T(8,128)(2,1)S(1)} %get-tuple-element.94), channel_id=1, source_target_pairs={{0,1},{1,0},{2,3},{3,2},{4,5},{5,4},{6,7},{7,6},{8,9},{9,8},{10,11... | collective-permute-start | bytes 1622024 | tf_op jit(solution)/shard_map/ppermute | solution.py:27
  227.3 3.5 %collective-permute-start.18 = (bf16[132,1024]{1,0:T(8,128)(2,1)S(1)}, bf16[132,1024]{1,0:T(8,128)(2,1)S(1)}, u32[]{:S(2)}, u32[]{:S(2)}) collective-permute-start(bf16[132,1024]{1,0:T(8,128)(2,1)S(1)} %slice.349), channel_id=1, source_target_pairs={{0,1},{1,0},{2,3},{3,2},{4,5},{5,4},{6,7},{7,6},{8,9},{9,8},{10,11... | collective-permute-start | bytes 811016 | tf_op jit(solution)/shard_map/ppermute | solution.py:27
  230.7 75.6 %collective-permute-start.25 = (bf16[8,1024]{1,0:T(8,128)(2,1)S(1)}, bf16[8,1024]{1,0:T(8,128)(2,1)S(1)}, u32[]{:S(2)}, u32[]{:S(2)}) collective-permute-start(bf16[8,1024]{1,0:T(8,128)(2,1)S(1)} %pad_maximum_fusion.8), channel_id=1, source_target_pairs={{0,32},{1,33},{2,34},{3,35},{4,36},{5,37},{6,38},{7,39},{8,40},{9,... | collective-permute-start | bytes 49160 | tf_op jit(solution)/shard_map/ppermute | solution.py:27
  244.1 12.5 %collective-permute-start.19 = (bf16[64,1024]{1,0:T(8,128)(2,1)S(1)}, bf16[64,1024]{1,0:T(8,128)(2,1)S(1)}, u32[]{:S(2)}, u32[]{:S(2)}) collective-permute-start(bf16[64,1024]{1,0:T(8,128)(2,1)S(1)} %pad_maximum_fusion.4), channel_id=1, source_target_pairs={{0,62},{1,3},{2,0},{3,5},{4,2},{5,7},{6,4},{7,9},{8,6},{9,11},{10,... | collective-permute-start | bytes 393224 | tf_op jit(solution)/shard_map/ppermute | solution.py:27
  248.3 8.5 %collective-permute-start.20 = (bf16[64,1024]{1,0:T(8,128)(2,1)S(1)}, bf16[64,1024]{1,0:T(8,128)(2,1)S(1)}, u32[]{:S(2)}, u32[]{:S(2)}) collective-permute-start(bf16[64,1024]{1,0:T(8,128)(2,1)S(1)} %pad_maximum_fusion.5), channel_id=1, source_target_pairs={{0,60},{1,5},{2,62},{3,7},{4,0},{5,9},{6,2},{7,11},{8,4},{9,13},{1... | collective-permute-start | bytes 393224 | tf_op jit(solution)/shard_map/ppermute | solution.py:27
  252.4 10.0 %collective-permute-start.21 = (bf16[64,1024]{1,0:T(8,128)(2,1)S(1)}, bf16[64,1024]{1,0:T(8,128)(2,1)S(1)}, u32[]{:S(2)}, u32[]{:S(2)}) collective-permute-start(bf16[64,1024]{1,0:T(8,128)(2,1)S(1)} %pad_maximum_fusion.6), channel_id=1, source_target_pairs={{0,58},{1,7},{2,60},{3,9},{4,62},{5,11},{6,0},{7,13},{8,2},{9,15},... | collective-permute-start | bytes 393224 | tf_op jit(solution)/shard_map/ppermute | solution.py:27
  262.4 49.2 %copy-start = (bf16[128,4096]{1,0:T(8,128)(2,1)S(1)}, bf16[128,4096]{1,0:T(8,128)(2,1)}, u32[]{:S(2)}) copy-start(bf16[128,4096]{1,0:T(8,128)(2,1)} %param.7) | copy-start | bytes 3145732
  262.8 20.5 %collective-permute-start.22 = (bf16[48,1024]{1,0:T(8,128)(2,1)S(1)}, bf16[48,1024]{1,0:T(8,128)(2,1)S(1)}, u32[]{:S(2)}, u32[]{:S(2)}) collective-permute-start(bf16[48,1024]{1,0:T(8,128)(2,1)S(1)} %get-tuple-element.75), channel_id=1, source_target_pairs={{0,56},{1,9},{2,58},{3,11},{4,60},{5,13},{6,62},{7,15},{8,0},{9,17... | collective-permute-start | bytes 294920 | tf_op jit(solution)/shard_map/ppermute | solution.py:27
  267.7 38.5 %collective-permute-start.24 = (bf16[48,1024]{1,0:T(8,128)(2,1)S(1)}, bf16[48,1024]{1,0:T(8,128)(2,1)S(1)}, u32[]{:S(2)}, u32[]{:S(2)}) collective-permute-start(bf16[48,1024]{1,0:T(8,128)(2,1)S(1)} %get-tuple-element.73), channel_id=1, source_target_pairs={{0,40},{1,25},{2,42},{3,27},{4,44},{5,29},{6,46},{7,31},{8,48},{9,... | collective-permute-start | bytes 294920 | tf_op jit(solution)/shard_map/ppermute | solution.py:27
  275.9 30.4 %collective-permute-start.23 = (bf16[48,1024]{1,0:T(8,128)(2,1)S(1)}, bf16[48,1024]{1,0:T(8,128)(2,1)S(1)}, u32[]{:S(2)}, u32[]{:S(2)}) collective-permute-start(bf16[48,1024]{1,0:T(8,128)(2,1)S(1)} %get-tuple-element.74), channel_id=1, source_target_pairs={{0,48},{1,17},{2,50},{3,19},{4,52},{5,21},{6,54},{7,23},{8,56},{9,... | collective-permute-start | bytes 294920 | tf_op jit(solution)/shard_map/ppermute | solution.py:27
  306.6 5.0 %collective-permute-start.26 = (bf16[128,1024]{1,0:T(8,128)(2,1)S(1)}, bf16[128,1024]{1,0:T(8,128)(2,1)S(1)}, u32[]{:S(2)}, u32[]{:S(2)}) collective-permute-start(bf16[128,1024]{1,0:T(8,128)(2,1)S(1)} %convolution_convert_fusion.7), channel_id=1, source_target_pairs={{0,1},{1,0},{2,3},{3,2},{4,5},{5,4},{6,7},{7,6},{8,9},{9,8},{10,11... | collective-permute-start | bytes 786440 | tf_op jit(solution)/shard_map/ppermute | solution.py:27
  311.6 14.9 %copy-start.3 = (f32[128]{0:T(128)S(1)}, f32[128]{0:T(128)}, u32[]{:S(2)}) copy-start(f32[128]{0:T(128)} %param.9) | copy-start | bytes 1540
  312.4 14.1 %collective-permute-start.27 = (bf16[128,1024]{1,0:T(8,128)(2,1)}, bf16[128,1024]{1,0:T(8,128)(2,1)S(1)}, u32[]{:S(2)}, u32[]{:S(2)}) collective-permute-start(bf16[128,1024]{1,0:T(8,128)(2,1)} %get-tuple-element.105), channel_id=1, source_target_pairs={{64,0},{128,64},{192,128},{256,192},{320,256},{384,320},{448,384},... | collective-permute-start | bytes 786440 | tf_op jit(solution)/shard_map/ppermute | solution.py:218
